TPU v7x, 32 devices: a whole 2x2x4 slice. The times are simulated.
32 devices in a mesh: dp: 4 (over y, x), vocab: 8 (over z, core).
Axes of the slice: x: 2, y: 2, z: 4, core: 2. Of those that a mesh axis runs over, the one named last changes fastest.
Arguments:
- hidden: bfloat16 [32, 4608], P('vocab', 'dp'), may hold values from -64 to 64
- embedding: bfloat16 [32768, 4608], P('vocab', 'dp'), may hold values from -4 to 4
- embed_cot: bfloat16 [32, 4608], P('vocab', 'dp'), may hold values from -0.059814453 to 0.059814453
- input_ids: int32 [32], replicated, may hold values from 0 to 32767
- target_ids: int32 [32], replicated, may hold values from 0 to 32767
- seq_of_token: int32 [32], replicated, may hold values from 0 to 7, never falling along the last dimension, each value on 1 to 8 neighbouring positions
- list_of_seq: int32 [8], replicated, may hold values from 0 to 1, as said below
- rank_of_seq: int32 [8], replicated, may hold values from 0 to 3, as said below
Outputs:
- table_grad: bfloat16 [32768, 4608], P('vocab', 'dp')
- hidden_grad: float32 [32, 4608], P('vocab', 'dp')
Inputs may be any that keep to these rules, and one draw needn't show every extreme that they name: `list_of_seq`: each of the 2 lists holds exactly 4 sequences. `rank_of_seq`: the sequences of one list carry the ranks 0 to 3, each once; rank 0 is preferred most.
All inputs are finite; a program needn't handle non-finite values.
Results may differ from a plain program's by a relative error of at most 0.0034.
Values may be sent and summed in bfloat16 or wider, within the bound.
No kernel may reach another device: no remote copies, remote signals or barrier semaphores. Data moves between devices by JAX's collectives and lax.ppermute only.
A program may use at most 64 MiB of HBM per device.

v0:
```python
import math

import jax
import jax.numpy as jnp
from jax import lax
from jax.sharding import PartitionSpec as P

D = 4608


preference_scale = 0.5


def merged(value, axis, join):
    pieces = jax.tree.map(lambda part: lax.all_gather(part, axis), value)
    head = jax.tree.map(lambda part: part[0], pieces)
    tail = jax.tree.map(lambda part: part[1:], pieces)
    so_far, _ = lax.scan(lambda so_far, slab: (join(so_far, slab), None), head, tail)
    return so_far


def pair_combine(earlier, latter):
    row_max = jnp.maximum(earlier[0], latter[0])
    row_sum = earlier[1] * jnp.exp(earlier[0] - row_max) + latter[1] * jnp.exp(latter[0] - row_max)
    return (row_max, row_sum)


def normalize(logits, targets, offset):
    local_max = jnp.max(logits, axis=1)
    local_sum = jnp.sum(jnp.exp(logits - local_max[:, None]), axis=1)
    columns = lax.broadcasted_iota(jnp.int32, logits.shape, 1) + offset
    target_hit = columns == targets[:, None]
    local_pick = jnp.sum(jnp.where(target_hit, logits, 0.0), axis=1)
    row_max, row_sum = merged((local_max, local_sum), "vocab", pair_combine)
    picked = lax.psum(local_pick, "vocab")
    log_norm = row_max + jnp.log(row_sum)
    return (log_norm, picked - log_norm, target_hit)


def list_coef(scores, list_of_seq, rank_of_seq):
    scaled = preference_scale * scores
    same_list = list_of_seq[:, None] == list_of_seq[None, :]
    in_suffix = same_list & (rank_of_seq[None, :] >= rank_of_seq[:, None])
    suffix_max = jnp.max(jnp.where(in_suffix, scaled[None, :], scaled[:, None]), axis=1)
    suffix_sum = jnp.sum(
        jnp.where(in_suffix, jnp.exp(jnp.minimum(scaled[None, :] - suffix_max[:, None], 0.0)), 0.0),
        axis=1,
    )
    suffix_lse = suffix_max + jnp.log(suffix_sum)
    portion = jnp.where(
        in_suffix, jnp.exp(jnp.minimum(scaled[None, :] - suffix_lse[:, None], 0.0)), 0.0
    )
    return preference_scale * (jnp.sum(portion, axis=0) - 1.0)


def logit_grad(logits, log_norm, target_hit, scores, list_of_seq, rank_of_seq, seq_hot):
    weight = jnp.sum(seq_hot * list_coef(scores, list_of_seq, rank_of_seq)[:, None], axis=0)
    return (
        weight[:, None] * (target_hit.astype(jnp.float32) - jnp.exp(logits - log_norm[:, None]))
    ).astype(jnp.bfloat16)


def body(
    hidden, embedding, embed_cot, input_ids, target_ids, seq_of_token, list_of_seq, rank_of_seq
):
    vocab_rows = embedding.shape[0]
    seq_count = list_of_seq.shape[0]
    offset = lax.axis_index("vocab") * vocab_rows
    hidden_all, cot_all = (
        lax.all_gather(hidden, "vocab", axis=0, tiled=True),
        lax.all_gather(embed_cot, "vocab", axis=0, tiled=True),
    )
    token_count = hidden_all.shape[0]
    entries = offset + lax.broadcasted_iota(jnp.int32, (vocab_rows, token_count), 0)
    input_hot = (entries == input_ids[None, :]).astype(jnp.bfloat16)
    input_part = jnp.dot(input_hot, cot_all, preferred_element_type=jnp.float32) * math.sqrt(D)
    seq_hot = (
        seq_of_token[None, :] == lax.broadcasted_iota(jnp.int32, (seq_count, token_count), 0)
    ).astype(jnp.float32)
    partial_value = jnp.einsum(
        "td,vd->tv", hidden_all, embedding, preferred_element_type=jnp.float32
    )
    logits = lax.psum(partial_value, "dp")
    log_norm, logprob, target_hit = normalize(logits, target_ids, offset)
    scores = jnp.sum(seq_hot * logprob[None, :], axis=1)
    grad_logits = logit_grad(
        logits, log_norm, target_hit, scores, list_of_seq, rank_of_seq, seq_hot
    )
    hidden_part = jnp.dot(grad_logits, embedding, preferred_element_type=jnp.float32)
    head_part = jnp.einsum("tv,td->vd", grad_logits, hidden_all, preferred_element_type=jnp.float32)
    hidden_grad = lax.psum_scatter(hidden_part, "vocab", scatter_dimension=0, tiled=True)
    table_grad = (head_part + input_part).astype(jnp.bfloat16)
    return (table_grad, hidden_grad)


def solution(mesh):
    placed = (P("vocab", "dp"), P("vocab", "dp"), P("vocab", "dp"), P(), P(), P(), P(), P())
    return jax.shard_map(
        body,
        mesh=mesh,
        in_specs=placed,
        out_specs=(P("vocab", "dp"), P("vocab", "dp")),
        check_vma=False,
    )
```

profile of v0, /device:TPU:0, one launch (start us, length us, event | category | flops | bytes accessed | tf_op | source)
XLA Modules:
  0.0 162.0 jit_solution(6815073787222578405)
XLA Ops:
  7.2 0.0 copy-start.5
  7.2 0.0 copy-start.4
  7.2 0.0 copy-start.3
  7.2 0.0 copy-start.7
  7.2 0.0 copy-start.1
  7.2 0.0 copy-start.2
  7.2 0.0 all-reduce.7.cloned.1.call-start
  7.3 16.0 %all-gather.2 = bf16[8,4,1152]{2,1,0:T(4,128)(2,1)S(1)} all-gather(bf16[1,4,1152]{2,1,0:T(4,128)(2,1)} %bitcast.24), channel_id=1, replica_groups=mesh['dp'=4,'vocab'=8] {'vocab'}, dimensions={0}, use_global_device_ids=true | all-gather | bytes 82944 | tf_op jit(solution)/shard_map/all_gather | solution.py:70
  23.3 7.4 %fusion.21 = f32[32,4096]{1,0:T(8,128)} fusion(bf16[32,1152]{1,0:T(8,128)(2,1)S(1)} %reshape.47, bf16[4096,1152]{1,0:T(8,128)(2,1)} %param.11), kind=kOutput, calls=%fused_computation.37 | convolution fusion | flops 301989888 | bytes 10035200 | tf_op jit(solution)/shard_map/td,vd->tv/dot_general | solution.py:80
  30.7 0.0 all-reduce.7.cloned.1.call-update
  30.7 0.0 all-reduce.9.cloned.1.call-start
  30.8 0.0 copy-done.4
  30.8 14.0 %all-gather.3 = bf16[8,4,1152]{2,1,0:T(4,128)(2,1)S(1)} all-gather(bf16[1,4,1152]{2,1,0:T(4,128)(2,1)S(1)} %bitcast.25), channel_id=1, replica_groups=mesh['dp'=4,'vocab'=8] {'vocab'}, dimensions={0}, use_global_device_ids=true | all-gather | bytes 82944 | tf_op jit(solution)/shard_map/all_gather | solution.py:71
  44.8 0.0 copy-done.5
  44.8 0.6 fusion.20
  46.6 30.6 %all-reduce.7.cloned.1.call-done = f32[32,4096]{1,0:T(8,128)} async-done(((f32[32,4096]{1,0:T(8,128)}), f32[32,4096]{1,0:T(8,128)}) %all-reduce.7.cloned.1.call-update) | async-done | bytes 524304 | tf_op jit(solution)/shard_map/psum | solution.py:83
  77.3 1.2 reduce_max.18
  78.4 0.2 dynamic-update-slice
  78.7 0.0 copy-done.3
  78.7 1.3 fusion.7
  80.0 0.2 dynamic-update-slice.1
  80.3 15.8 %all-reduce.3 = (f32[256]{0:T(256)S(1)}, f32[256]{0:T(256)S(1)}, f32[32]{0:T(128)S(1)}) all-reduce(f32[256]{0:T(256)S(1)} %dynamic-update-slice, f32[256]{0:T(256)S(1)} %dynamic-update-slice.1, f32[32]{0:T(128)S(1)} %get-tuple-element.32), channel_id=2, replica_groups=mesh['dp'=4,'vocab'=8] {'vocab'}, use_global_device_ids=true, to_apply=%add | all-reduce | flops 544 | bytes 4352
  96.1 0.1 slice.18
  96.2 0.1 slice.19
  96.3 0.1 reshape.39
  96.3 0.1 reshape.38
  96.4 0.3 while.12
  96.7 0.0 copy-done.7
  96.7 0.1 select_reduce_fusion.4
  96.8 0.0 copy-done.1
  96.8 0.0 copy-done.2
  96.8 0.2 select_reduce_fusion.3
  97.0 0.2 select_reduce_fusion.2
  97.2 0.1 select_reduce_fusion.1
  97.3 0.1 select_reduce_fusion
  97.4 0.0 copy-start
  97.4 6.3 %fusion.14 = f32[32,1152]{1,0:T(8,128)} fusion(bf16[4096,1152]{1,0:T(8,128)(2,1)} %param.11, f32[32,4096]{1,0:T(8,128)} %all-reduce.7.cloned.1.call-done, f32[32]{0:T(128)S(1)} %get-tuple-element.50, f32[32]{0:T(128)S(1)} %select_reduce_fusion, s32[4096]{0:T(1024)S(1)} %iota_add_fusion, s32[32]{0:T(128)S(1)} %copy-done.3), kind=kOutput, calls=%fused_computation.33 | convolution fusion | flops 302776320 | bytes 10125696 | tf_op jit(solution)/shard_map/dot_general | solution.py:89
  103.7 0.0 all-reduce.9.cloned.1.call-update
  103.8 0.0 copy-done
  103.8 0.0 copy-start.6
  103.8 8.0 %fusion.16 = f32[4096,1152]{1,0:T(8,128)} fusion(bf16[32,1152]{1,0:T(8,128)(2,1)S(1)} %reshape.47, f32[32,4096]{1,0:T(8,128)S(1)} %copy-done, f32[32]{0:T(128)S(1)} %get-tuple-element.50, f32[32]{0:T(128)S(1)} %select_reduce_fusion, s32[4096]{0:T(1024)S(1)} %iota_add_fusion, s32[32]{0:T(128)S(1)} %copy-done.3), kind=kOutput, calls=%fused_computation.34 | convolution fusion | flops 302776320 | bytes 19489152 | tf_op jit(solution)/shard_map/tv,td->vd/dot_general | solution.py:90
  111.8 0.0 copy-done.6
  111.8 10.6 %fusion.6 = bf16[4096,1152]{1,0:T(8,128)(2,1)} fusion(f32[4096,1152]{1,0:T(8,128)} %fusion.16, bf16[32,1152]{1,0:T(8,128)(2,1)S(1)} %reshape.49, s32[4096]{0:T(1024)S(1)} %iota_add_fusion, s32[32]{0:T(128)S(1)} %copy-done.6), kind=kOutput, calls=%fused_computation.9 | convolution fusion | flops 316276736 | bytes 28401792 | tf_op jit(solution)/shard_map/dot_general | solution.py:76
  122.4 31.4 %all-reduce.9.cloned.1.call-done = f32[32,1152]{1,0:T(8,128)} async-done(((f32[32,1152]{1,0:T(8,128)}), f32[32,1152]{1,0:T(8,128)}) %all-reduce.9.cloned.1.call-update) | async-done | bytes 147472
  153.8 1.4 constant_dynamic-slice_fusion.2
  (18 shorter events, 0.3 us)
Async XLA Ops:
  7.2 37.6 %copy-start.5 = (u32[32]{0:T(128)S(1)}, u32[32]{0:T(128)}, u32[]{:S(2)}) copy-start(u32[32]{0:T(128)} %constant.34) | copy-start | bytes 388
  7.2 23.6 %copy-start.4 = (bf16[4,1152]{1,0:T(4,128)(2,1)S(1)}, bf16[4,1152]{1,0:T(4,128)(2,1)}, u32[]{:S(2)}) copy-start(bf16[4,1152]{1,0:T(4,128)(2,1)} %param.12) | copy-start | bytes 27652
  7.2 71.5 %copy-start.3 = (s32[32]{0:T(128)S(1)}, s32[32]{0:T(128)}, u32[]{:S(2)}) copy-start(s32[32]{0:T(128)} %param.14) | copy-start | bytes 388
  7.2 89.5 %copy-start.7 = (s32[32]{0:T(128)S(1)}, s32[32]{0:T(128)}, u32[]{:S(2)}) copy-start(s32[32]{0:T(128)} %param.15) | copy-start | bytes 388
  7.2 89.6 %copy-start.1 = (s32[8]{0:T(128)S(1)}, s32[8]{0:T(128)}, u32[]{:S(2)}) copy-start(s32[8]{0:T(128)} %param.17) | copy-start | bytes 100
  7.2 89.6 %copy-start.2 = (s32[8]{0:T(128)S(1)}, s32[8]{0:T(128)}, u32[]{:S(2)}) copy-start(s32[8]{0:T(128)} %param.16) | copy-start | bytes 100
  7.2 70.0 %all-reduce.7.cloned.1.call-start = ((), (), s32[]{:S(2)}) async-start(), calls=%async_computation | async-start | bytes 1048576 | tf_op jit(solution)/shard_map/psum | solution.py:83
  30.7 123.1 %all-reduce.9.cloned.1.call-start = ((), (), s32[]{:S(2)}) async-start(), calls=%async_computation.1 | async-start | bytes 294912
  97.4 6.4 %copy-start = (f32[32,4096]{1,0:T(8,128)S(1)}, f32[32,4096]{1,0:T(8,128)}, u32[]{:S(2)}) copy-start(f32[32,4096]{1,0:T(8,128)} %all-reduce.7.cloned.1.call-done) | copy-start | bytes 1572868
  103.8 8.0 %copy-start.6 = (s32[32]{0:T(128)S(1)}, s32[32]{0:T(128)}, u32[]{:S(2)}) copy-start(s32[32]{0:T(128)} %param.13) | copy-start | bytes 388
Sparse Core Ops, SparseCore 0:
  30.8 46.3 all-reduce.6
  103.9 49.8 all-reduce.8
where the time goes:
time: 162 us
  waiting for transfers between devices  62 us (38%)
  blocking collectives  45.8 us (28%)
  matrix products  32.3 us (20%)
  between operations  15.4 us (10%)
  other arithmetic  3.4 us (2%)
  local copies, waits for them, and re-layouts  2.85 us (2%)
    unnamed x3, waiting for transfers between devices  31.4 us
    psum x1, waiting for transfers between devices, body(): logits = lax.psum(partial_value, 'dp')  30.6 us
    all_gather x1, blocking collectives, body(): lax.all_gather(hidden, 'vocab', axis=0, tiled=True)  16 us
    unnamed x1, blocking collectives  15.8 us
    all_gather x1, blocking collectives, body(): lax.all_gather(embed_cot, 'vocab', axis=0, tiled=True)  14 us
    dot_general x1, matrix products, body(): jnp.dot(input_hot, cot_all, preferred_element_type=jnp.float32)  10.6 us
    dot_general x1, matrix products, body(): jnp.einsum('tv,td->vd', grad_logits, hidden_all, preferred_element_type=j...  8.03 us
    dot_general x1, matrix products, body(): jnp.einsum('td,vd->tv', hidden_all, embedding, preferred_element_type=jnp...  7.35 us
  transfers between devices with their start and end apart: 2, of which 2 were waited for; matrix products, arithmetic and copies ran while one was open for 12% of the time, Pallas kernels for 0%

commit v1 on v0

v1 whole, which is shorter than its diff:
```python
import functools
import math

import jax
import jax.numpy as jnp
from jax import lax
from jax.experimental import pallas as pl
from jax.experimental.pallas import tpu as pltpu
from jax.sharding import PartitionSpec as P

f32 = jnp.float32
bf16 = jnp.bfloat16
preference_scale = 0.5
NT = (((1,), (1,)), ((), ()))
TN = (((0,), (0,)), ((), ()))
VM = pl.BlockSpec(memory_space=pltpu.VMEM)
LANES = 128


def swap(value, axis, size, k):
    return lax.ppermute(value, axis, [(i, i ^ k) for i in range(size)])


def halvings(size):
    ks = []
    k = size // 2
    while k:
        ks.append(k)
        k //= 2
    return ks


def doubled(value, axis, size):
    for k in halvings(size):
        value = jnp.concatenate([value, swap(value, axis, size, k)], axis=0)
    return value


def row_of_place(me, places, rows, size):
    block = places // rows
    owner = jnp.full_like(places, me)
    for r, k in enumerate(halvings(size)):
        owner = owner ^ (((block >> r) & 1) * k)
    return owner * rows + places % rows


def as_column(row, picked):
    return jnp.sum(jnp.where(picked, row, jnp.zeros_like(row)), axis=1, keepdims=True)


def place_mask(me, tokens, rows, size):
    here = row_of_place(me, lax.broadcasted_iota(jnp.int32, (tokens, tokens), 0), rows, size)
    return here == lax.broadcasted_iota(jnp.int32, (tokens, tokens), 1)


def ids_column(row, picked):
    return as_column(row.astype(f32), picked).astype(jnp.int32)


def logits_kernel(tile, h_ref, e_ref, a_ref, b_ref):
    half = a_ref.shape[1]
    for start in range(0, 2 * half, tile):
        part = lax.dot_general(
            e_ref[pl.ds(start, tile), :], h_ref[...], NT, preferred_element_type=f32
        )
        ref, at = (a_ref, start) if start < half else (b_ref, start - half)
        ref[:, pl.ds(at, tile)] = part.T


def stats_kernel(size, rows, parts, me_ref, tgt_ref, *refs):
    ins, (l_ref, s_ref) = refs[:-2], refs[-2:]
    tokens, width = l_ref.shape
    half = width // 2
    me = me_ref[0]
    picked = place_mask(me, tokens, rows, size)
    target = ids_column(tgt_ref[...], picked)
    for n in range(2):
        total = ins[n * parts][...]
        for r in ins[n * parts + 1 : (n + 1) * parts]:
            total = total + r[...]
        l_ref[:, pl.ds(n * half, half)] = total
    logits = l_ref[...]
    columns = lax.broadcasted_iota(jnp.int32, logits.shape, 1) + me * width
    top = jnp.max(logits, axis=1, keepdims=True)
    total = jnp.sum(jnp.exp(logits - top), axis=1, keepdims=True)
    pick = jnp.sum(jnp.where(columns == target, logits, 0.0), axis=1, keepdims=True)
    same = lax.broadcasted_iota(jnp.int32, (tokens, s_ref.shape[1]), 0) == lax.broadcasted_iota(
        jnp.int32, (tokens, s_ref.shape[1]), 1
    )
    s_ref[...] = jnp.zeros_like(s_ref)
    for n, column in enumerate((top, total, pick)):
        s_ref[n : n + 1, :] = jnp.sum(jnp.where(same, column, 0.0), axis=0, keepdims=True)


def join_kernel(step, mine_ref, other_ref, out_ref):
    width = mine_ref.shape[1]
    other = other_ref[...]
    lane = lax.broadcasted_iota(jnp.int32, other.shape, 1)
    other = jnp.where(
        (lane // step) % 2 == 1, pltpu.roll(other, step, 1), pltpu.roll(other, width - step, 1)
    )
    mine = mine_ref[...]
    top = jnp.maximum(mine[0:1, :], other[0:1, :])
    out_ref[...] = jnp.zeros_like(out_ref)
    out_ref[0:1, :] = top
    out_ref[1:2, :] = mine[1:2, :] * jnp.exp(mine[0:1, :] - top) + other[1:2, :] * jnp.exp(
        other[0:1, :] - top
    )
    out_ref[2:3, :] = mine[2:3, :] + other[2:3, :]


def list_coef(scaled, lists, ranks):
    count = scaled.shape[1]
    diagonal = lax.broadcasted_iota(jnp.int32, (count, count), 0) == lax.broadcasted_iota(
        jnp.int32, (count, count), 1
    )
    scaled_col = as_column(scaled, diagonal)
    list_col = as_column(lists, diagonal)
    rank_col = as_column(ranks, diagonal)
    in_suffix = (list_col == lists) & (ranks >= rank_col)
    top = jnp.max(jnp.where(in_suffix, scaled, scaled_col), axis=1, keepdims=True)
    total = jnp.sum(
        jnp.where(in_suffix, jnp.exp(jnp.minimum(scaled - top, 0.0)), 0.0), axis=1, keepdims=True
    )
    lse = top + jnp.log(total)
    portion = jnp.where(in_suffix, jnp.exp(jnp.minimum(scaled - lse, 0.0)), 0.0)
    return preference_scale * (jnp.sum(portion, axis=0, keepdims=True) - 1.0)


def grad_kernel(
    size, rows, me_ref, tgt_ref, seq_ref, list_ref, rank_ref, s_ref, l_ref, e_ref, g_ref, keep_ref, send_ref
):
    tokens, width = l_ref.shape
    seqs = list_ref.shape[1]
    me = me_ref[0]
    picked = place_mask(me, tokens, rows, size)
    target = ids_column(tgt_ref[...], picked)
    seq = ids_column(seq_ref[...], picked)
    same = lax.broadcasted_iota(jnp.int32, (tokens, s_ref.shape[1]), 0) == lax.broadcasted_iota(
        jnp.int32, (tokens, s_ref.shape[1]), 1
    )
    top, total, pick = (as_column(s_ref[n : n + 1, :], same) for n in range(3))
    log_norm = top + jnp.log(total)
    seq_hot = seq == lax.broadcasted_iota(jnp.int32, (tokens, seqs), 1)
    scores = jnp.sum(jnp.where(seq_hot, pick - log_norm, 0.0), axis=0, keepdims=True)
    coef = list_coef(
        preference_scale * scores, list_ref[...].astype(f32), rank_ref[...].astype(f32)
    )
    weight = as_column(coef, seq_hot)
    logits = l_ref[...]
    columns = lax.broadcasted_iota(jnp.int32, logits.shape, 1) + me * width
    hit = (columns == target).astype(f32)
    g_ref[...] = (weight * (hit - jnp.exp(logits - log_norm))).astype(bf16)
    part = jnp.dot(g_ref[...], e_ref[...], preferred_element_type=f32)
    keep_ref[...] = part[: tokens // 2]
    send_ref[...] = part[tokens // 2 :]


def bf16_terms(value, count=3):
    import numpy as np

    left, terms = np.float32(value), []
    for _ in range(count):
        term = np.float32(left.astype(jnp.bfloat16))
        terms.append(float(term))
        left = np.float32(left - term)
    return terms


def table_kernel(size, rows, terms, me_ref, ids_ref, g_ref, h_ref, c_ref, out_ref):
    tokens, tile = g_ref.shape
    me = me_ref[0]
    first = me * (tile * pl.num_programs(0)) + pl.program_id(0) * tile
    ids = ids_column(ids_ref[...], place_mask(me, tokens, rows, size))
    columns = lax.broadcasted_iota(jnp.int32, (tokens, tile), 1) + first
    hit = columns == ids
    left = jnp.concatenate(
        [g_ref[...]] + [jnp.where(hit, t, 0.0).astype(bf16) for t in terms], axis=0
    )
    right = jnp.concatenate([h_ref[...]] + [c_ref[...]] * len(terms), axis=0)
    out_ref[...] = lax.dot_general(left, right, TN, preferred_element_type=f32).astype(bf16)


def params(mib):
    return pltpu.CompilerParams(vmem_limit_bytes=mib << 20)


def body(
    hidden, embedding, embed_cot, input_ids, target_ids, seq_of_token, list_of_seq, rank_of_seq,
    *, n_dp, n_vocab, width_all,
):
    rows, depth = hidden.shape
    width = embedding.shape[0]
    half = width // 2
    tokens = rows * n_vocab
    seqs = list_of_seq.shape[0]
    tile = math.gcd(512, half)
    lanes = -(-tokens // LANES) * LANES
    me = lax.axis_index("vocab").astype(jnp.int32).reshape(1)
    smem = pl.BlockSpec(memory_space=pltpu.SMEM)
    tgt, ids, seq = (v.reshape(1, tokens) for v in (target_ids, input_ids, seq_of_token))
    lists, ranks = list_of_seq.reshape(1, seqs), rank_of_seq.reshape(1, seqs)
    table = pltpu.with_memory_space_constraint(embedding, pltpu.VMEM)

    hidden_all = doubled(hidden, "vocab", n_vocab)
    part_a, part_b = pl.pallas_call(
        functools.partial(logits_kernel, tile),
        in_specs=[VM, VM],
        out_specs=(VM, VM),
        out_shape=(jax.ShapeDtypeStruct((tokens, half), f32),) * 2,
        compiler_params=params(12),
        name="logits",
    )(hidden_all, table)

    cot_in, _, _ = lax.optimization_barrier((embed_cot, part_a, part_b))
    cot_all = doubled(cot_in, "vocab", n_vocab)

    order = halvings(n_dp)[::-1]
    pieces = [[part_a], [part_b]]
    for r in range(len(order)):
        ks = (order[r], order[-1 - r])
        others = [swap(sum(p[1:], p[0]), "dp", n_dp, k) for p, k in zip(pieces, ks)]
        pieces = [[sum(p[1:], p[0]), o] for p, o in zip(pieces, others)]
    parts = len(pieces[0])
    logits, stats = pl.pallas_call(
        functools.partial(stats_kernel, n_vocab, rows, parts),
        in_specs=[smem, VM] + [VM] * (2 * parts),
        out_specs=(VM, VM),
        out_shape=(
            jax.ShapeDtypeStruct((tokens, width), f32),
            jax.ShapeDtypeStruct((8, lanes), f32),
        ),
        compiler_params=params(12),
        name="stats",
    )(me, tgt, *pieces[0], *pieces[1])
    for r, k in enumerate(halvings(n_vocab)):
        stats = pl.pallas_call(
            functools.partial(join_kernel, rows << r),
            in_specs=[VM, VM],
            out_specs=VM,
            out_shape=jax.ShapeDtypeStruct(stats.shape, f32),
            compiler_params=params(2),
            name="join",
        )(stats, swap(stats, "vocab", n_vocab, k))

    grad, keep, send = pl.pallas_call(
        functools.partial(grad_kernel, n_vocab, rows),
        in_specs=[smem] + [VM] * 7,
        out_specs=(VM, VM, VM),
        out_shape=(
            jax.ShapeDtypeStruct((tokens, width), bf16),
            jax.ShapeDtypeStruct((tokens // 2, depth), f32),
            jax.ShapeDtypeStruct((tokens // 2, depth), f32),
        ),
        compiler_params=params(12),
        name="grad",
    )(me, tgt, seq, lists, ranks, stats, logits, table)

    back = halvings(n_vocab)[::-1]
    for n, k in enumerate(back):
        other = swap(send, "vocab", n_vocab, k)
        if n + 1 < len(back):
            cut = keep.shape[0] // 2
            send = keep[cut:] + other[cut:]
            keep = keep[:cut] + other[:cut]
        else:
            keep = keep + other
    block = math.gcd(1024, width)
    table_grad = pl.pallas_call(
        functools.partial(table_kernel, n_vocab, rows, bf16_terms(math.sqrt(width_all))),
        grid=(width // block,),
        in_specs=[
            smem,
            pl.BlockSpec((1, tokens), lambda i: (0, 0)),
            pl.BlockSpec((tokens, block), lambda i: (0, i)),
            pl.BlockSpec((tokens, depth), lambda i: (0, 0)),
            pl.BlockSpec((tokens, depth), lambda i: (0, 0)),
        ],
        out_specs=pl.BlockSpec((block, depth), lambda i: (i, 0)),
        out_shape=jax.ShapeDtypeStruct((width, depth), bf16),
        compiler_params=params(24),
        cost_estimate=pl.CostEstimate(
            flops=2 * 128 * width * depth, bytes_accessed=2 * width * depth, transcendentals=0
        ),
        name="table",
    )(me, ids, grad, hidden_all, cot_all)
    return (table_grad, keep)


def solution(mesh):
    n_dp, n_vocab = mesh.shape["dp"], mesh.shape["vocab"]
    placed = (P("vocab", "dp"), P("vocab", "dp"), P("vocab", "dp"), P(), P(), P(), P(), P())

    def whole(hidden, *rest):
        return jax.shard_map(
            functools.partial(body, n_dp=n_dp, n_vocab=n_vocab, width_all=hidden.shape[1]),
            mesh=mesh,
            in_specs=placed,
            out_specs=(P("vocab", "dp"), P("vocab", "dp")),
            check_vma=False,
        )(hidden, *rest)

    return whole
```

time: 162 us -> 68.8 us (0.42)
  blocking collectives: 45.8 us -> 0 us
  waiting for transfers between devices: 62 us -> 21.1 us
  matrix products: 32.3 us -> 0 us
  starting transfers between devices: 0.08 us -> 25.5 us
  between operations: 15.4 us -> 0.79 us
  Pallas kernels: 0 us -> 10.8 us
  local copies, waits for them, and re-layouts: 2.85 us -> 7.38 us
    dot_general x4 -> x0, matrix products: 32.3 us -> none  [the longest x1 10.6 us: body(): jnp.dot(input_hot, cot_all, preferred_element_type=jnp.float32)]
    unnamed x3 -> x0, waiting for transfers between devices: 31.4 us -> none
    psum x1 -> x0, waiting for transfers between devices: 30.6 us -> none  [body(): logits = lax.psum(partial_value, 'dp')]
    all_gather x2 -> x0, blocking collectives: 30 us -> none  [the longest x1 16 us: body(): lax.all_gather(hidden, 'vocab', axis=0, tiled=True)]
    ppermute x0 -> x16, starting transfers between devices: none -> 25.5 us  [swap(): return lax.ppermute(value, axis, [(i, i ^ k) for i in range(size)])]
    ppermute x0 -> x16, waiting for transfers between devices: none -> 21.1 us  [swap(): return lax.ppermute(value, axis, [(i, i ^ k) for i in range(size)])]
    unnamed x1 -> x0, blocking collectives: 15.8 us -> none
    pallas_call x0 -> x7, Pallas kernels: none -> 10.8 us  [the longest x1 5.53 us: body(): pl.pallas_call(functools.partial(table_kernel, n_vocab, rows, bf16_terms(...]
  transfers between devices with their start and end apart: 2 -> 16, of which waited for: 2 -> 10; matrix products, arithmetic and copies ran while one was open for 12% -> 0% of each run, Pallas kernels for 0% -> 12%
where the time goes in v1:
time: 68.8 us; the launch traced here: 68.5 us
  starting transfers between devices  25.5 us (37%)
  waiting for transfers between devices  21.1 us (31%)
  Pallas kernels  10.8 us (16%)
  local copies, waits for them, and re-layouts  7.38 us (11%)
  other arithmetic  2.91 us (4%)
  between operations  0.79 us (1%)
    ppermute x16, starting transfers between devices, swap(): return lax.ppermute(value, axis, [(i, i ^ k) for i in range(size)])  25.5 us
    ppermute x16, waiting for transfers between devices, swap(): return lax.ppermute(value, axis, [(i, i ^ k) for i in range(size)])  21.1 us
    unnamed x16, local copies, waits for them, and re-layouts  7.38 us
    pallas_call x1, Pallas kernels, body(): pl.pallas_call(functools.partial(table_kernel, n_vocab, rows, bf16_terms(...  5.53 us
    pallas_call x1, Pallas kernels, body(): pl.pallas_call(functools.partial(logits_kernel, tile), in_specs=[VM, VM],...  2.62 us
    concatenate x6, other arithmetic, doubled(): value = jnp.concatenate([value, swap(value, axis, size, k)], axis=0)  2.21 us
    pallas_call x1, Pallas kernels, body(): pl.pallas_call(functools.partial(grad_kernel, n_vocab, rows), in_specs=[s...  2.1 us
  transfers between devices with their start and end apart: 16, of which 10 were waited for; matrix products, arithmetic and copies ran while one was open for 0% of the time, Pallas kernels for 12%

profile of v1, /device:TPU:0, one launch (start us, length us, event | category | flops | bytes accessed | tf_op | source)
XLA Modules:
  0.0 68.5 jit_solution(11048817453598229536)
XLA Ops:
  0.6 0.0 copy-start.7
  0.7 4.1 %collective-permute-start = (bf16[4,1152]{1,0:T(4,128)(2,1)}, bf16[4,1152]{1,0:T(4,128)(2,1)S(1)}, u32[]{:S(2)}, u32[]{:S(2)}) collective-permute-start(bf16[4,1152]{1,0:T(4,128)(2,1)} %param.8), channel_id=1, source_target_pairs={{0,4},{1,5},{2,6},{3,7},{4,0},{5,1},{6,2},{7,3},{8,12},{9,13},{10,... | collective-permute-start | bytes 27656 | tf_op jit(solution)/shard_map/ppermute | solution.py:21
  4.8 1.9 %collective-permute-done = bf16[4,1152]{1,0:T(4,128)(2,1)S(1)} collective-permute-done((bf16[4,1152]{1,0:T(4,128)(2,1)}, bf16[4,1152]{1,0:T(4,128)(2,1)S(1)}, u32[]{:S(2)}, u32[]{:S(2)}) %collective-permute-start) | collective-permute-done | bytes 9248 | tf_op jit(solution)/shard_map/ppermute | solution.py:21
  6.7 0.7 %pad_maximum_fusion.4 = bf16[8,1152]{1,0:T(8,128)(2,1)S(1)} fusion(bf16[4,1152]{1,0:T(4,128)(2,1)S(1)} %collective-permute-done, bf16[4,1152]{1,0:T(4,128)(2,1)} %param.8), kind=kLoop, calls=%fused_computation.9 | loop fusion | flops 36864 | bytes 36864 | tf_op jit(solution)/shard_map/concatenate | solution.py:35
  7.4 2.0 %collective-permute-start.1 = (bf16[8,1152]{1,0:T(8,128)(2,1)S(1)}, bf16[8,1152]{1,0:T(8,128)(2,1)S(1)}, u32[]{:S(2)}, u32[]{:S(2)}) collective-permute-start(bf16[8,1152]{1,0:T(8,128)(2,1)S(1)} %pad_maximum_fusion.4), channel_id=1, source_target_pairs={{0,2},{1,3},{2,0},{3,1},{4,6},{5,7},{6,4},{7,5},{8,10},{9,11},{10,... | collective-permute-start | bytes 55304 | tf_op jit(solution)/shard_map/ppermute | solution.py:21
  9.4 1.9 %collective-permute-done.1 = bf16[8,1152]{1,0:T(8,128)(2,1)S(1)} collective-permute-done((bf16[8,1152]{1,0:T(8,128)(2,1)S(1)}, bf16[8,1152]{1,0:T(8,128)(2,1)S(1)}, u32[]{:S(2)}, u32[]{:S(2)}) %collective-permute-start.1) | collective-permute-done | bytes 18464 | tf_op jit(solution)/shard_map/ppermute | solution.py:21
  11.2 0.7 %pad_maximum_fusion.2 = bf16[16,1152]{1,0:T(8,128)(2,1)S(1)} fusion(bf16[8,1152]{1,0:T(8,128)(2,1)S(1)} %collective-permute-done.1, bf16[4,1152]{1,0:T(4,128)(2,1)S(1)} %collective-permute-done, bf16[4,1152]{1,0:T(4,128)(2,1)} %param.8), kind=kLoop, calls=%fused_computation.4 | loop fusion | flops 110592 | bytes 73728 | tf_op jit(solution)/shard_map/concatenate | solution.py:35
  11.9 0.1 collective-permute-start.2
  12.0 1.2 %collective-permute-done.2 = bf16[16,1152]{1,0:T(8,128)(2,1)S(1)} collective-permute-done((bf16[16,1152]{1,0:T(8,128)(2,1)S(1)}, bf16[16,1152]{1,0:T(8,128)(2,1)S(1)}, u32[]{:S(2)}, u32[]{:S(2)}) %collective-permute-start.2) | collective-permute-done | bytes 36896 | tf_op jit(solution)/shard_map/ppermute | solution.py:21
  13.2 0.7 %pad_maximum_fusion.h_ref = bf16[32,1152]{1,0:T(8,128)(2,1)S(1)} fusion(bf16[16,1152]{1,0:T(8,128)(2,1)S(1)} %collective-permute-done.2, bf16[8,1152]{1,0:T(8,128)(2,1)S(1)} %collective-permute-done.1, bf16[4,1152]{1,0:T(4,128)(2,1)S(1)} %collective-permute-done, bf16[4,1152]{1,0:T(4,128)(2,1)} %param.8), kind=kLoop, calls=%fused_computation | loop fusion | flops 294912 | bytes 147456 | tf_op jit(solution)/shard_map/concatenate | solution.py:35
  13.9 0.0 copy-start
  13.9 3.7 %copy-done = bf16[4096,1152]{1,0:T(8,128)(2,1)S(1)} copy-done((bf16[4096,1152]{1,0:T(8,128)(2,1)S(1)}, bf16[4096,1152]{1,0:T(8,128)(2,1)}, u32[]{:S(2)}) %copy-start) | copy-done | bytes 9437208
  17.6 2.6 %logits.1 = (f32[32,2048]{1,0:T(8,128)S(1)}, f32[32,2048]{1,0:T(8,128)S(1)}) custom-call(bf16[32,1152]{1,0:T(8,128)(2,1)S(1)} %pad_maximum_fusion.h_ref, bf16[4096,1152]{1,0:T(8,128)(2,1)S(1)} %copy-done), custom_call_target="tpu_custom_call" | custom-call | tf_op jit(solution)/shard_map/logits/pallas_call | solution.py:206
  20.3 1.9 %collective-permute-start.3 = (f32[32,2048]{1,0:T(8,128)S(1)}, f32[32,2048]{1,0:T(8,128)S(1)}, u32[]{:S(2)}, u32[]{:S(2)}) collective-permute-start(f32[32,2048]{1,0:T(8,128)S(1)} %get-tuple-element.10), channel_id=1, source_target_pairs={{0,8},{8,0},{16,24},{24,16},{1,9},{9,1},{17,25},{25,17},{2,10},{10... | collective-permute-start | bytes 786440 | tf_op jit(solution)/shard_map/ppermute | solution.py:21
  22.1 1.5 %collective-permute-start.5 = (f32[32,2048]{1,0:T(8,128)S(1)}, f32[32,2048]{1,0:T(8,128)S(1)}, u32[]{:S(2)}, u32[]{:S(2)}) collective-permute-start(f32[32,2048]{1,0:T(8,128)S(1)} %get-tuple-element.11), channel_id=1, source_target_pairs={{0,16},{8,24},{16,0},{24,8},{1,17},{9,25},{17,1},{25,9},{2,18},{10... | collective-permute-start | bytes 786440 | tf_op jit(solution)/shard_map/ppermute | solution.py:21
  23.7 5.1 %collective-permute-done.3 = f32[32,2048]{1,0:T(8,128)S(1)} collective-permute-done((f32[32,2048]{1,0:T(8,128)S(1)}, f32[32,2048]{1,0:T(8,128)S(1)}, u32[]{:S(2)}, u32[]{:S(2)}) %collective-permute-start.3) | collective-permute-done | bytes 262176 | tf_op jit(solution)/shard_map/ppermute | solution.py:21
  28.8 1.8 %collective-permute-start.4 = (f32[32,2048]{1,0:T(8,128)S(1)}, f32[32,2048]{1,0:T(8,128)S(1)}, u32[]{:S(2)}, u32[]{:S(2)}) collective-permute-start(f32[32,2048]{1,0:T(8,128)S(1)} %add.23.refs_0_), channel_id=1, source_target_pairs={{0,16},{8,24},{16,0},{24,8},{1,17},{9,25},{17,1},{25,9},{2,18},{10... | collective-permute-start | bytes 786440 | tf_op jit(solution)/shard_map/ppermute | solution.py:21
  30.6 0.0 collective-permute-done.5
  30.7 1.5 %collective-permute-start.6 = (f32[32,2048]{1,0:T(8,128)S(1)}, f32[32,2048]{1,0:T(8,128)S(1)}, u32[]{:S(2)}, u32[]{:S(2)}) collective-permute-start(f32[32,2048]{1,0:T(8,128)S(1)} %add.24.refs_2_), channel_id=1, source_target_pairs={{0,8},{8,0},{16,24},{24,16},{1,9},{9,1},{17,25},{25,17},{2,10},{10... | collective-permute-start | bytes 786440 | tf_op jit(solution)/shard_map/ppermute | solution.py:21
  32.2 2.6 %collective-permute-start.10 = (bf16[4,1152]{1,0:T(4,128)(2,1)S(1)}, bf16[4,1152]{1,0:T(4,128)(2,1)S(1)}, u32[]{:S(2)}, u32[]{:S(2)}) collective-permute-start(bf16[4,1152]{1,0:T(4,128)(2,1)S(1)} %copy-done.7), channel_id=1, source_target_pairs={{0,4},{1,5},{2,6},{3,7},{4,0},{5,1},{6,2},{7,3},{8,12},{9,13},{10,... | collective-permute-start | bytes 27656 | tf_op jit(solution)/shard_map/ppermute | solution.py:21
  34.8 2.0 %collective-permute-done.10 = bf16[4,1152]{1,0:T(4,128)(2,1)S(1)} collective-permute-done((bf16[4,1152]{1,0:T(4,128)(2,1)S(1)}, bf16[4,1152]{1,0:T(4,128)(2,1)S(1)}, u32[]{:S(2)}, u32[]{:S(2)}) %collective-permute-start.10) | collective-permute-done | bytes 9248 | tf_op jit(solution)/shard_map/ppermute | solution.py:21
  36.8 1.6 %collective-permute-start.11 = (bf16[8,1152]{1,0:T(8,128)(2,1)S(1)}, bf16[8,1152]{1,0:T(8,128)(2,1)S(1)}, u32[]{:S(2)}, u32[]{:S(2)}) collective-permute-start(bf16[8,1152]{1,0:T(8,128)(2,1)S(1)} %pad_maximum_fusion.5), channel_id=1, source_target_pairs={{0,2},{1,3},{2,0},{3,1},{4,6},{5,7},{6,4},{7,5},{8,10},{9,11},{10,... | collective-permute-start | bytes 55304 | tf_op jit(solution)/shard_map/ppermute | solution.py:21
  38.5 0.0 collective-permute-done.4.refs_1_
  38.5 0.0 collective-permute-done.6.refs_3_
  38.5 0.4 stats.1
  38.8 2.7 %collective-permute-start.7 = (f32[8,128]{1,0:T(8,128)S(1)}, f32[8,128]{1,0:T(8,128)S(1)}, u32[]{:S(2)}, u32[]{:S(2)}) collective-permute-start(f32[8,128]{1,0:T(8,128)S(1)} %get-tuple-element.12.mine_ref), channel_id=1, source_target_pairs={{0,4},{1,5},{2,6},{3,7},{4,0},{5,1},{6,2},{7,3},{8,12},{9,13},{10,... | collective-permute-start | bytes 12296 | tf_op jit(solution)/shard_map/ppermute | solution.py:21
  41.5 1.9 %collective-permute-done.7.other_ref = f32[8,128]{1,0:T(8,128)S(1)} collective-permute-done((f32[8,128]{1,0:T(8,128)S(1)}, f32[8,128]{1,0:T(8,128)S(1)}, u32[]{:S(2)}, u32[]{:S(2)}) %collective-permute-start.7) | collective-permute-done | bytes 4128 | tf_op jit(solution)/shard_map/ppermute | solution.py:21
  43.4 0.1 join.3.mine_ref
  43.5 1.1 %collective-permute-start.8 = (f32[8,128]{1,0:T(8,128)S(1)}, f32[8,128]{1,0:T(8,128)S(1)}, u32[]{:S(2)}, u32[]{:S(2)}) collective-permute-start(f32[8,128]{1,0:T(8,128)S(1)} %join.3.mine_ref), channel_id=1, source_target_pairs={{0,2},{1,3},{2,0},{3,1},{4,6},{5,7},{6,4},{7,5},{8,10},{9,11},{10,... | collective-permute-start | bytes 12296 | tf_op jit(solution)/shard_map/ppermute | solution.py:21
  44.6 2.5 %collective-permute-done.8.other_ref = f32[8,128]{1,0:T(8,128)S(1)} collective-permute-done((f32[8,128]{1,0:T(8,128)S(1)}, f32[8,128]{1,0:T(8,128)S(1)}, u32[]{:S(2)}, u32[]{:S(2)}) %collective-permute-start.8) | collective-permute-done | bytes 4128 | tf_op jit(solution)/shard_map/ppermute | solution.py:21
  47.1 0.1 join.4.mine_ref
  47.2 0.0 collective-permute-start.9
  47.2 1.2 %collective-permute-done.9.other_ref = f32[8,128]{1,0:T(8,128)S(1)} collective-permute-done((f32[8,128]{1,0:T(8,128)S(1)}, f32[8,128]{1,0:T(8,128)S(1)}, u32[]{:S(2)}, u32[]{:S(2)}) %collective-permute-start.9) | collective-permute-done | bytes 4128 | tf_op jit(solution)/shard_map/ppermute | solution.py:21
  48.4 0.1 join.5.s_ref
  48.5 0.0 copy-start.1
  48.5 3.7 %copy-done.1 = bf16[4096,1152]{1,0:T(8,128)(2,1)S(1)} copy-done((bf16[4096,1152]{1,0:T(8,128)(2,1)S(1)}, bf16[4096,1152]{1,0:T(8,128)(2,1)}, u32[]{:S(2)}) %copy-start.1) | copy-done | bytes 9437208
  52.2 2.1 %grad.1 = (bf16[32,4096]{1,0:T(8,128)(2,1)S(1)}, f32[16,1152]{1,0:T(8,128)S(1)}, f32[16,1152]{1,0:T(8,128)S(1)}) custom-call(s32[1]{0:T(128)} %bitcast.me_ref, s32[1,32]{1,0:T(1,128)S(1)} %bitcast.7, s32[1,32]{1,0:T(1,128)S(1)} %bitcast.9, s32[1,8]{1,0:T(1,128)S(1)} %bitcast.10, s32[1,8]{1,0:T(1,128)S(1)} %bitcast.11, f32[8,128]{1,0:T(8,128)S(1)} %join.5.s_ref, ...), custom_call_target="tpu_custom_call" | custom-call | tf_op jit(solution)/shard_map/grad/pallas_call | solution.py:246
  54.3 0.2 collective-permute-start.13
  54.5 0.0 collective-permute-done.11
  54.5 0.4 collective-permute-start.12
  54.9 0.7 collective-permute-done.13
  55.6 1.2 %collective-permute-start.14 = (f32[8,1152]{1,0:T(8,128)S(1)}, f32[8,1152]{1,0:T(8,128)S(1)}, u32[]{:S(2)}, u32[]{:S(2)}) collective-permute-start(f32[8,1152]{1,0:T(8,128)S(1)} %get-tuple-element.19), channel_id=1, source_target_pairs={{0,2},{1,3},{2,0},{3,1},{4,6},{5,7},{6,4},{7,5},{8,10},{9,11},{10,... | collective-permute-start | bytes 110600 | tf_op jit(solution)/shard_map/ppermute | solution.py:21
  56.8 0.0 collective-permute-done.12
  56.8 2.8 %collective-permute-done.14 = f32[8,1152]{1,0:T(8,128)S(1)} collective-permute-done((f32[8,1152]{1,0:T(8,128)S(1)}, f32[8,1152]{1,0:T(8,128)S(1)}, u32[]{:S(2)}, u32[]{:S(2)}) %collective-permute-start.14) | collective-permute-done | bytes 36896 | tf_op jit(solution)/shard_map/ppermute | solution.py:21
  59.7 2.7 %collective-permute-start.15 = (f32[4,1152]{1,0:T(4,128)S(1)}, f32[4,1152]{1,0:T(4,128)S(1)}, u32[]{:S(2)}, u32[]{:S(2)}) collective-permute-start(f32[4,1152]{1,0:T(4,128)S(1)} %slice_add_fusion.2), channel_id=1, source_target_pairs={{0,4},{1,5},{2,6},{3,7},{4,0},{5,1},{6,2},{7,3},{8,12},{9,13},{10,... | collective-permute-start | bytes 55304 | tf_op jit(solution)/shard_map/ppermute | solution.py:21
  62.3 5.5 %table.1 = bf16[4096,1152]{1,0:T(8,128)(2,1)} custom-call(s32[1]{0:T(128)} %bitcast.me_ref, s32[1,32]{1,0:T(1,128)S(1)} %bitcast.8, bf16[32,4096]{1,0:T(8,128)(2,1)S(1)} %get-tuple-element.14.g_ref, bf16[32,1152]{1,0:T(8,128)(2,1)S(1)} %pad_maximum_fusion.h_ref, bf16[32,1152]{1,0:T(8,128)(2,1)S(1)} %pad_maximum_fusion.1.c_ref), custom_call_target="tpu_custom_call" | custom-call | flops 1207959552 | bytes 9437184 | tf_op jit(solution)/shard_map/table/pallas_call | solution.py:269
  67.8 0.0 collective-permute-done.15
  67.9 0.6 fusion
  (18 shorter events, 0.2 us)
Async XLA Ops:
  0.6 31.6 %copy-start.7 = (bf16[4,1152]{1,0:T(4,128)(2,1)S(1)}, bf16[4,1152]{1,0:T(4,128)(2,1)}, u32[]{:S(2)}) copy-start(bf16[4,1152]{1,0:T(4,128)(2,1)} %param.10) | copy-start | bytes 27652
  0.6 37.8 %copy-start.2 = (s32[32]{0:T(128)S(1)}, s32[32]{0:T(128)}, u32[]{:S(2)}) copy-start(s32[32]{0:T(128)} %param.12) | copy-start | bytes 388
  0.7 47.8 %copy-start.6 = (s32[8]{0:T(128)S(1)}, s32[8]{0:T(128)}, u32[]{:S(2)}) copy-start(s32[8]{0:T(128)} %param.15) | copy-start | bytes 100
  0.7 47.8 %copy-start.5 = (s32[8]{0:T(128)S(1)}, s32[8]{0:T(128)}, u32[]{:S(2)}) copy-start(s32[8]{0:T(128)} %param.14) | copy-start | bytes 100
  0.7 47.8 %copy-start.4 = (s32[32]{0:T(128)S(1)}, s32[32]{0:T(128)}, u32[]{:S(2)}) copy-start(s32[32]{0:T(128)} %param.13) | copy-start | bytes 388
  0.7 6.0 %collective-permute-start = (bf16[4,1152]{1,0:T(4,128)(2,1)}, bf16[4,1152]{1,0:T(4,128)(2,1)S(1)}, u32[]{:S(2)}, u32[]{:S(2)}) collective-permute-start(bf16[4,1152]{1,0:T(4,128)(2,1)} %param.8), channel_id=1, source_target_pairs={{0,4},{1,5},{2,6},{3,7},{4,0},{5,1},{6,2},{7,3},{8,12},{9,13},{10,... | collective-permute-start | bytes 27656 | tf_op jit(solution)/shard_map/ppermute | solution.py:21
  7.4 3.8 %collective-permute-start.1 = (bf16[8,1152]{1,0:T(8,128)(2,1)S(1)}, bf16[8,1152]{1,0:T(8,128)(2,1)S(1)}, u32[]{:S(2)}, u32[]{:S(2)}) collective-permute-start(bf16[8,1152]{1,0:T(8,128)(2,1)S(1)} %pad_maximum_fusion.4), channel_id=1, source_target_pairs={{0,2},{1,3},{2,0},{3,1},{4,6},{5,7},{6,4},{7,5},{8,10},{9,11},{10,... | collective-permute-start | bytes 55304 | tf_op jit(solution)/shard_map/ppermute | solution.py:21
  11.9 1.3 %collective-permute-start.2 = (bf16[16,1152]{1,0:T(8,128)(2,1)S(1)}, bf16[16,1152]{1,0:T(8,128)(2,1)S(1)}, u32[]{:S(2)}, u32[]{:S(2)}) collective-permute-start(bf16[16,1152]{1,0:T(8,128)(2,1)S(1)} %pad_maximum_fusion.2), channel_id=1, source_target_pairs={{0,1},{1,0},{2,3},{3,2},{4,5},{5,4},{6,7},{7,6},{8,9},{9,8},{10,11... | collective-permute-start | bytes 110600 | tf_op jit(solution)/shard_map/ppermute | solution.py:21
  13.9 3.7 %copy-start = (bf16[4096,1152]{1,0:T(8,128)(2,1)S(1)}, bf16[4096,1152]{1,0:T(8,128)(2,1)}, u32[]{:S(2)}) copy-start(bf16[4096,1152]{1,0:T(8,128)(2,1)} %e_ref.3) | copy-start | bytes 28311556
  17.6 44.7 %copy-start.3 = (s32[32]{0:T(128)S(1)}, s32[32]{0:T(128)}, u32[]{:S(2)}) copy-start(s32[32]{0:T(128)} %param.11) | copy-start | bytes 388
  20.3 8.5 %collective-permute-start.3 = (f32[32,2048]{1,0:T(8,128)S(1)}, f32[32,2048]{1,0:T(8,128)S(1)}, u32[]{:S(2)}, u32[]{:S(2)}) collective-permute-start(f32[32,2048]{1,0:T(8,128)S(1)} %get-tuple-element.10), channel_id=1, source_target_pairs={{0,8},{8,0},{16,24},{24,16},{1,9},{9,1},{17,25},{25,17},{2,10},{10... | collective-permute-start | bytes 786440 | tf_op jit(solution)/shard_map/ppermute | solution.py:21
  22.1 8.5 %collective-permute-start.5 = (f32[32,2048]{1,0:T(8,128)S(1)}, f32[32,2048]{1,0:T(8,128)S(1)}, u32[]{:S(2)}, u32[]{:S(2)}) collective-permute-start(f32[32,2048]{1,0:T(8,128)S(1)} %get-tuple-element.11), channel_id=1, source_target_pairs={{0,16},{8,24},{16,0},{24,8},{1,17},{9,25},{17,1},{25,9},{2,18},{10... | collective-permute-start | bytes 786440 | tf_op jit(solution)/shard_map/ppermute | solution.py:21
  28.8 9.7 %collective-permute-start.4 = (f32[32,2048]{1,0:T(8,128)S(1)}, f32[32,2048]{1,0:T(8,128)S(1)}, u32[]{:S(2)}, u32[]{:S(2)}) collective-permute-start(f32[32,2048]{1,0:T(8,128)S(1)} %add.23.refs_0_), channel_id=1, source_target_pairs={{0,16},{8,24},{16,0},{24,8},{1,17},{9,25},{17,1},{25,9},{2,18},{10... | collective-permute-start | bytes 786440 | tf_op jit(solution)/shard_map/ppermute | solution.py:21
  30.7 7.8 %collective-permute-start.6 = (f32[32,2048]{1,0:T(8,128)S(1)}, f32[32,2048]{1,0:T(8,128)S(1)}, u32[]{:S(2)}, u32[]{:S(2)}) collective-permute-start(f32[32,2048]{1,0:T(8,128)S(1)} %add.24.refs_2_), channel_id=1, source_target_pairs={{0,8},{8,0},{16,24},{24,16},{1,9},{9,1},{17,25},{25,17},{2,10},{10... | collective-permute-start | bytes 786440 | tf_op jit(solution)/shard_map/ppermute | solution.py:21
  32.2 4.6 %collective-permute-start.10 = (bf16[4,1152]{1,0:T(4,128)(2,1)S(1)}, bf16[4,1152]{1,0:T(4,128)(2,1)S(1)}, u32[]{:S(2)}, u32[]{:S(2)}) collective-permute-start(bf16[4,1152]{1,0:T(4,128)(2,1)S(1)} %copy-done.7), channel_id=1, source_target_pairs={{0,4},{1,5},{2,6},{3,7},{4,0},{5,1},{6,2},{7,3},{8,12},{9,13},{10,... | collective-permute-start | bytes 27656 | tf_op jit(solution)/shard_map/ppermute | solution.py:21
  36.8 17.7 %collective-permute-start.11 = (bf16[8,1152]{1,0:T(8,128)(2,1)S(1)}, bf16[8,1152]{1,0:T(8,128)(2,1)S(1)}, u32[]{:S(2)}, u32[]{:S(2)}) collective-permute-start(bf16[8,1152]{1,0:T(8,128)(2,1)S(1)} %pad_maximum_fusion.5), channel_id=1, source_target_pairs={{0,2},{1,3},{2,0},{3,1},{4,6},{5,7},{6,4},{7,5},{8,10},{9,11},{10,... | collective-permute-start | bytes 55304 | tf_op jit(solution)/shard_map/ppermute | solution.py:21
  38.8 4.6 %collective-permute-start.7 = (f32[8,128]{1,0:T(8,128)S(1)}, f32[8,128]{1,0:T(8,128)S(1)}, u32[]{:S(2)}, u32[]{:S(2)}) collective-permute-start(f32[8,128]{1,0:T(8,128)S(1)} %get-tuple-element.12.mine_ref), channel_id=1, source_target_pairs={{0,4},{1,5},{2,6},{3,7},{4,0},{5,1},{6,2},{7,3},{8,12},{9,13},{10,... | collective-permute-start | bytes 12296 | tf_op jit(solution)/shard_map/ppermute | solution.py:21
  43.5 3.6 %collective-permute-start.8 = (f32[8,128]{1,0:T(8,128)S(1)}, f32[8,128]{1,0:T(8,128)S(1)}, u32[]{:S(2)}, u32[]{:S(2)}) collective-permute-start(f32[8,128]{1,0:T(8,128)S(1)} %join.3.mine_ref), channel_id=1, source_target_pairs={{0,2},{1,3},{2,0},{3,1},{4,6},{5,7},{6,4},{7,5},{8,10},{9,11},{10,... | collective-permute-start | bytes 12296 | tf_op jit(solution)/shard_map/ppermute | solution.py:21
  47.2 1.2 %collective-permute-start.9 = (f32[8,128]{1,0:T(8,128)S(1)}, f32[8,128]{1,0:T(8,128)S(1)}, u32[]{:S(2)}, u32[]{:S(2)}) collective-permute-start(f32[8,128]{1,0:T(8,128)S(1)} %join.4.mine_ref), channel_id=1, source_target_pairs={{0,1},{1,0},{2,3},{3,2},{4,5},{5,4},{6,7},{7,6},{8,9},{9,8},{10,11... | collective-permute-start | bytes 12296 | tf_op jit(solution)/shard_map/ppermute | solution.py:21
  48.5 3.7 %copy-start.1 = (bf16[4096,1152]{1,0:T(8,128)(2,1)S(1)}, bf16[4096,1152]{1,0:T(8,128)(2,1)}, u32[]{:S(2)}) copy-start(bf16[4096,1152]{1,0:T(8,128)(2,1)} %e_ref.3) | copy-start | bytes 28311556
  54.3 1.3 %collective-permute-start.13 = (f32[16,1152]{1,0:T(8,128)S(1)}, f32[16,1152]{1,0:T(8,128)S(1)}, u32[]{:S(2)}, u32[]{:S(2)}) collective-permute-start(f32[16,1152]{1,0:T(8,128)S(1)} %get-tuple-element.17), channel_id=1, source_target_pairs={{0,1},{1,0},{2,3},{3,2},{4,5},{5,4},{6,7},{7,6},{8,9},{9,8},{10,11... | collective-permute-start | bytes 221192 | tf_op jit(solution)/shard_map/ppermute | solution.py:21
  54.5 2.3 %collective-permute-start.12 = (bf16[16,1152]{1,0:T(8,128)(2,1)S(1)}, bf16[16,1152]{1,0:T(8,128)(2,1)S(1)}, u32[]{:S(2)}, u32[]{:S(2)}) collective-permute-start(bf16[16,1152]{1,0:T(8,128)(2,1)S(1)} %pad_maximum_fusion.3), channel_id=1, source_target_pairs={{0,1},{1,0},{2,3},{3,2},{4,5},{5,4},{6,7},{7,6},{8,9},{9,8},{10,11... | collective-permute-start | bytes 110600 | tf_op jit(solution)/shard_map/ppermute | solution.py:21
  55.6 4.0 %collective-permute-start.14 = (f32[8,1152]{1,0:T(8,128)S(1)}, f32[8,1152]{1,0:T(8,128)S(1)}, u32[]{:S(2)}, u32[]{:S(2)}) collective-permute-start(f32[8,1152]{1,0:T(8,128)S(1)} %get-tuple-element.19), channel_id=1, source_target_pairs={{0,2},{1,3},{2,0},{3,1},{4,6},{5,7},{6,4},{7,5},{8,10},{9,11},{10,... | collective-permute-start | bytes 110600 | tf_op jit(solution)/shard_map/ppermute | solution.py:21
  59.7 8.2 %collective-permute-start.15 = (f32[4,1152]{1,0:T(4,128)S(1)}, f32[4,1152]{1,0:T(4,128)S(1)}, u32[]{:S(2)}, u32[]{:S(2)}) collective-permute-start(f32[4,1152]{1,0:T(4,128)S(1)} %slice_add_fusion.2), channel_id=1, source_target_pairs={{0,4},{1,5},{2,6},{3,7},{4,0},{5,1},{6,2},{7,3},{8,12},{9,13},{10,... | collective-permute-start | bytes 55304 | tf_op jit(solution)/shard_map/ppermute | solution.py:21

commit v2 on v1

--- a/solution.py
+++ b/solution.py
@@ -30,10 +30,100 @@
     return ks
 
 
-def doubled(value, axis, size):
-    for k in halvings(size):
-        value = jnp.concatenate([value, swap(value, axis, size, k)], axis=0)
-    return value
+def joined_kernel(pieces, *refs):
+    out_ref = refs[-1]
+    at = 0
+    for ref in refs[:pieces]:
+        rows = ref.shape[0]
+        out_ref[at : at + rows, :] = ref[...]
+        at += rows
+
+
+def joined(pieces, extra=()):
+    rows = sum(p.shape[0] for p in pieces)
+    return pl.pallas_call(
+        functools.partial(joined_kernel, len(pieces)),
+        in_specs=[VM] * len(pieces) + [pl.BlockSpec(memory_space=pl.ANY)] * len(extra),
+        out_specs=VM,
+        out_shape=jax.ShapeDtypeStruct((rows,) + pieces[0].shape[1:], pieces[0].dtype),
+        compiler_params=params(2),
+        name="joined",
+    )(*pieces, *extra)
+
+
+def paired_kernel(h_ref, c_ref, out_ref, h_buf, c_buf, sems):
+    depth = h_ref.shape[1]
+    gap = out_ref.shape[1] // 2
+    bufs = (h_buf, c_buf)
+    copies = [
+        pltpu.make_async_copy(ref, buf, sems.at[n])
+        for n, (ref, buf) in enumerate(zip((h_ref, c_ref), bufs))
+    ]
+    for copy in copies:
+        copy.start()
+    if gap != depth:
+        out_ref[...] = jnp.zeros_like(out_ref)
+    for n, copy in enumerate(copies):
+        copy.wait()
+        out_ref[:, n * gap : n * gap + depth] = bufs[n][...]
+
+
+def paired(hidden, cot, gap):
+    return pl.pallas_call(
+        paired_kernel,
+        in_specs=[pl.BlockSpec(memory_space=pltpu.HBM)] * 2,
+        out_specs=VM,
+        out_shape=jax.ShapeDtypeStruct((hidden.shape[0], 2 * gap), hidden.dtype),
+        scratch_shapes=[
+            pltpu.VMEM(hidden.shape, hidden.dtype),
+            pltpu.VMEM(cot.shape, cot.dtype),
+            pltpu.SemaphoreType.DMA((2,)),
+        ],
+        compiler_params=params(2),
+        name="paired",
+    )(in_hbm(hidden), in_hbm(cot))
+
+
+def added_kernel(a_ref, b_ref, out_ref):
+    out_ref[...] = a_ref[...] + b_ref[...]
+
+
+def added(pieces):
+    if len(pieces) == 1:
+        return pieces[0]
+    return pl.pallas_call(
+        added_kernel,
+        in_specs=[VM, VM],
+        out_specs=VM,
+        out_shape=jax.ShapeDtypeStruct(pieces[0].shape, pieces[0].dtype),
+        compiler_params=params(4),
+        name="added",
+    )(*pieces)
+
+
+def in_hbm(value):
+    return pltpu.with_memory_space_constraint(value, pltpu.HBM)
+
+
+def fetch_kernel(start, e_ref, after_ref, out_ref, sem):
+    copy = pltpu.make_async_copy(e_ref.at[pl.ds(start, out_ref.shape[0]), :], out_ref, sem)
+    copy.start()
+    copy.wait()
+
+
+def fetched(table, start, rows, after):
+    return pl.pallas_call(
+        functools.partial(fetch_kernel, start),
+        in_specs=[pl.BlockSpec(memory_space=pltpu.HBM), pl.BlockSpec(memory_space=pl.ANY)],
+        out_specs=VM,
+        out_shape=jax.ShapeDtypeStruct((rows, table.shape[1]), table.dtype),
+        scratch_shapes=[pltpu.SemaphoreType.DMA],
+        compiler_params=params(2),
+        cost_estimate=pl.CostEstimate(
+            flops=0, bytes_accessed=2 * rows * table.shape[1] * 2, transcendentals=0
+        ),
+        name="fetched",
+    )(table, after)
 
 
 def row_of_place(me, places, rows, size):
@@ -57,21 +147,37 @@
     return as_column(row.astype(f32), picked).astype(jnp.int32)
 
 
-def logits_kernel(tile, h_ref, e_ref, a_ref, b_ref):
-    half = a_ref.shape[1]
-    for start in range(0, 2 * half, tile):
-        part = lax.dot_general(
-            e_ref[pl.ds(start, tile), :], h_ref[...], NT, preferred_element_type=f32
-        )
-        ref, at = (a_ref, start) if start < half else (b_ref, start - half)
-        ref[:, pl.ds(at, tile)] = part.T
-
-
-def stats_kernel(size, rows, parts, me_ref, tgt_ref, *refs):
+def logits_kernel(tile, count, h_ref, *refs):
+    depth = refs[0].shape[1]
+    a_ref = refs[count]
+    at = 0
+    for e_ref in refs[:count]:
+        for start in range(0, e_ref.shape[0], tile):
+            part = lax.dot_general(
+                e_ref[pl.ds(start, tile), :],
+                h_ref[:, :depth],
+                NT,
+                preferred_element_type=f32,
+            )
+            a_ref[:, pl.ds(at, tile)] = part.T
+            at += tile
+
+
+def logits_fetch_kernel(tile, count, start, h_ref, *refs):
+    table_ref, last_ref, sem = refs[count], refs[count + 2], refs[count + 3]
+    copy = pltpu.make_async_copy(
+        table_ref.at[pl.ds(start, last_ref.shape[0]), :], last_ref, sem
+    )
+    copy.start()
+    logits_kernel(tile, count, h_ref, *refs[:count], refs[count + 1])
+    copy.wait()
+
+
+def stats_kernel(size, rows, parts, tgt_ref, *refs):
     ins, (l_ref, s_ref) = refs[:-2], refs[-2:]
     tokens, width = l_ref.shape
     half = width // 2
-    me = me_ref[0]
+    me = lax.axis_index("vocab")
     picked = place_mask(me, tokens, rows, size)
     target = ids_column(tgt_ref[...], picked)
     for n in range(2):
@@ -128,11 +234,12 @@
 
 
 def grad_kernel(
-    size, rows, me_ref, tgt_ref, seq_ref, list_ref, rank_ref, s_ref, l_ref, e_ref, g_ref, keep_ref, send_ref
+    size, rows, count, tgt_ref, seq_ref, list_ref, rank_ref, s_ref, l_ref, *refs
 ):
+    e_refs, (g_ref, keep_ref, send_ref) = refs[:count], refs[count:]
     tokens, width = l_ref.shape
     seqs = list_ref.shape[1]
-    me = me_ref[0]
+    me = lax.axis_index("vocab")
     picked = place_mask(me, tokens, rows, size)
     target = ids_column(tgt_ref[...], picked)
     seq = ids_column(seq_ref[...], picked)
@@ -151,7 +258,13 @@
     columns = lax.broadcasted_iota(jnp.int32, logits.shape, 1) + me * width
     hit = (columns == target).astype(f32)
     g_ref[...] = (weight * (hit - jnp.exp(logits - log_norm))).astype(bf16)
-    part = jnp.dot(g_ref[...], e_ref[...], preferred_element_type=f32)
+    part, at = None, 0
+    for e_ref in e_refs:
+        piece = jnp.dot(
+            g_ref[:, pl.ds(at, e_ref.shape[0])], e_ref[...], preferred_element_type=f32
+        )
+        part = piece if part is None else part + piece
+        at += e_ref.shape[0]
     keep_ref[...] = part[: tokens // 2]
     send_ref[...] = part[tokens // 2 :]
 
@@ -167,18 +280,31 @@
     return terms
 
 
-def table_kernel(size, rows, terms, me_ref, ids_ref, g_ref, h_ref, c_ref, out_ref):
-    tokens, tile = g_ref.shape
-    me = me_ref[0]
-    first = me * (tile * pl.num_programs(0)) + pl.program_id(0) * tile
-    ids = ids_column(ids_ref[...], place_mask(me, tokens, rows, size))
-    columns = lax.broadcasted_iota(jnp.int32, (tokens, tile), 1) + first
-    hit = columns == ids
-    left = jnp.concatenate(
-        [g_ref[...]] + [jnp.where(hit, t, 0.0).astype(bf16) for t in terms], axis=0
-    )
-    right = jnp.concatenate([h_ref[...]] + [c_ref[...]] * len(terms), axis=0)
-    out_ref[...] = lax.dot_general(left, right, TN, preferred_element_type=f32).astype(bf16)
+def table_kernel(size, rows, terms, tile, ids_ref, g_ref, hc_ref, out_ref, buf, sems):
+    tokens, width = g_ref.shape
+    depth = out_ref.shape[1]
+    gap = hc_ref.shape[1] // 2
+    me = lax.axis_index("vocab")
+    ids = ids_column(ids_ref[...], place_mask(me, tokens, rows, size)) - me * width
+    right = jnp.concatenate(
+        [hc_ref[:, :depth]] + [hc_ref[:, gap : gap + depth]] * len(terms), axis=0
+    )
+    copies = []
+    for n in range(width // tile):
+        hit = lax.broadcasted_iota(jnp.int32, (tokens, tile), 1) + n * tile == ids
+        left = jnp.concatenate(
+            [g_ref[:, pl.ds(n * tile, tile)]]
+            + [jnp.where(hit, t, 0.0).astype(bf16) for t in terms],
+            axis=0,
+        )
+        buf[pl.ds(n * tile, tile), :] = lax.dot_general(
+            left, right, TN, preferred_element_type=f32
+        ).astype(bf16)
+        at = pl.ds(n * tile, tile)
+        copies.append(pltpu.make_async_copy(buf.at[at], out_ref.at[at], sems.at[n]))
+        copies[-1].start()
+    for copy in copies:
+        copy.wait()
 
 
 def params(mib):
@@ -196,35 +322,63 @@
     seqs = list_of_seq.shape[0]
     tile = math.gcd(512, half)
     lanes = -(-tokens // LANES) * LANES
-    me = lax.axis_index("vocab").astype(jnp.int32).reshape(1)
-    smem = pl.BlockSpec(memory_space=pltpu.SMEM)
     tgt, ids, seq = (v.reshape(1, tokens) for v in (target_ids, input_ids, seq_of_token))
     lists, ranks = list_of_seq.reshape(1, seqs), rank_of_seq.reshape(1, seqs)
-    table = pltpu.with_memory_space_constraint(embedding, pltpu.VMEM)
-
-    hidden_all = doubled(hidden, "vocab", n_vocab)
-    part_a, part_b = pl.pallas_call(
-        functools.partial(logits_kernel, tile),
-        in_specs=[VM, VM],
+    gap = -(-depth // LANES) * LANES
+    quarter = width // 4
+    embedding = in_hbm(embedding)
+
+    gathered = [paired(hidden, embed_cot, gap)]
+    after, fetches = gathered[0], []
+    for n, k in enumerate(halvings(n_vocab)):
+        other = swap(after, "vocab", n_vocab, k)
+        if len(fetches) < 3:
+            fetches.append(fetched(embedding, len(fetches) * quarter, quarter, after))
+            after = joined(gathered + [other], fetches[-1:])
+        else:
+            after = joined(gathered + [other])
+        gathered = [after]
+    both = after
+    while len(fetches) < 3:
+        fetches.append(fetched(embedding, len(fetches) * quarter, quarter, after))
+    part_a, last = pl.pallas_call(
+        functools.partial(logits_fetch_kernel, tile, 2, 3 * quarter),
+        in_specs=[VM] * 3 + [pl.BlockSpec(memory_space=pltpu.HBM)],
         out_specs=(VM, VM),
-        out_shape=(jax.ShapeDtypeStruct((tokens, half), f32),) * 2,
+        out_shape=(
+            jax.ShapeDtypeStruct((tokens, half), f32),
+            jax.ShapeDtypeStruct((quarter, depth), bf16),
+        ),
+        scratch_shapes=[pltpu.SemaphoreType.DMA],
         compiler_params=params(12),
-        name="logits",
-    )(hidden_all, table)
-
-    cot_in, _, _ = lax.optimization_barrier((embed_cot, part_a, part_b))
-    cot_all = doubled(cot_in, "vocab", n_vocab)
+        name="logits_a",
+    )(both, *fetches[:2], embedding)
+    table = [*fetches, last]
+    part_b = pl.pallas_call(
+        functools.partial(logits_kernel, tile, 2),
+        in_specs=[VM] * 3,
+        out_specs=VM,
+        out_shape=jax.ShapeDtypeStruct((tokens, half), f32),
+        compiler_params=params(12),
+        name="logits_b",
+    )(both, *table[2:])
 
     order = halvings(n_dp)[::-1]
     pieces = [[part_a], [part_b]]
     for r in range(len(order)):
         ks = (order[r], order[-1 - r])
-        others = [swap(sum(p[1:], p[0]), "dp", n_dp, k) for p, k in zip(pieces, ks)]
-        pieces = [[sum(p[1:], p[0]), o] for p, o in zip(pieces, others)]
+        pairs = [
+            (d * n_vocab + v, (d ^ ks[v % 2]) * n_vocab + v)
+            for d in range(n_dp)
+            for v in range(n_vocab)
+        ]
+        for n in range(2):
+            total = added(pieces[n])
+            pieces[n] = [total, lax.ppermute(total, ("dp", "vocab"), pairs)]
     parts = len(pieces[0])
     logits, stats = pl.pallas_call(
         functools.partial(stats_kernel, n_vocab, rows, parts),
-        in_specs=[smem, VM] + [VM] * (2 * parts),
+        in_specs=[VM] * (1 + 2 * parts),
         out_specs=(VM, VM),
         out_shape=(
             jax.ShapeDtypeStruct((tokens, width), f32),
@@ -232,7 +386,7 @@
         ),
         compiler_params=params(12),
         name="stats",
-    )(me, tgt, *pieces[0], *pieces[1])
+    )(tgt, *pieces[0], *pieces[1])
     for r, k in enumerate(halvings(n_vocab)):
         stats = pl.pallas_call(
             functools.partial(join_kernel, rows << r),
@@ -244,8 +398,8 @@
         )(stats, swap(stats, "vocab", n_vocab, k))
 
     grad, keep, send = pl.pallas_call(
-        functools.partial(grad_kernel, n_vocab, rows),
-        in_specs=[smem] + [VM] * 7,
+        functools.partial(grad_kernel, n_vocab, rows, len(table)),
+        in_specs=[VM] * (6 + len(table)),
         out_specs=(VM, VM, VM),
         out_shape=(
             jax.ShapeDtypeStruct((tokens, width), bf16),
@@ -254,7 +408,7 @@
         ),
         compiler_params=params(12),
         name="grad",
-    )(me, tgt, seq, lists, ranks, stats, logits, table)
+    )(tgt, seq, lists, ranks, stats, logits, *table)
 
     back = halvings(n_vocab)[::-1]
     for n, k in enumerate(back):
@@ -265,25 +419,22 @@
             keep = keep[:cut] + other[:cut]
         else:
             keep = keep + other
-    block = math.gcd(1024, width)
+    block = math.gcd(512, width)
     table_grad = pl.pallas_call(
-        functools.partial(table_kernel, n_vocab, rows, bf16_terms(math.sqrt(width_all))),
-        grid=(width // block,),
-        in_specs=[
-            smem,
-            pl.BlockSpec((1, tokens), lambda i: (0, 0)),
-            pl.BlockSpec((tokens, block), lambda i: (0, i)),
-            pl.BlockSpec((tokens, depth), lambda i: (0, 0)),
-            pl.BlockSpec((tokens, depth), lambda i: (0, 0)),
+        functools.partial(table_kernel, n_vocab, rows, bf16_terms(math.sqrt(width_all)), block),
+        in_specs=[VM, VM, VM],
+        out_specs=pl.BlockSpec(memory_space=pltpu.HBM),
+        out_shape=jax.ShapeDtypeStruct((width, depth), bf16),
+        scratch_shapes=[
+            pltpu.VMEM((width, depth), bf16),
+            pltpu.SemaphoreType.DMA((width // block,)),
         ],
-        out_specs=pl.BlockSpec((block, depth), lambda i: (i, 0)),
-        out_shape=jax.ShapeDtypeStruct((width, depth), bf16),
         compiler_params=params(24),
         cost_estimate=pl.CostEstimate(
             flops=2 * 128 * width * depth, bytes_accessed=2 * width * depth, transcendentals=0
         ),
         name="table",
-    )(me, ids, grad, hidden_all, cot_all)
+    )(ids, grad, both)
     return (table_grad, keep)
 
 

time: 68.8 us -> 58.2 us (0.85)
  local copies, waits for them, and re-layouts: 7.38 us -> 0.03 us
  Pallas kernels: 10.8 us -> 16 us
  waiting for transfers between devices: 21.1 us -> 17.8 us
  starting transfers between devices: 25.5 us -> 22.6 us
  other arithmetic: 2.91 us -> 0.64 us
    ppermute x16 -> x9, waiting for transfers between devices: 21.1 us -> 8.09 us  [swap(): return lax.ppermute(value, axis, [(i, i ^ k) for i in range(size)])]
    ppermute x0 -> x4, waiting for transfers between devices: none -> 9.76 us  [body(): pieces[n] = [total, lax.ppermute(total, ('dp', 'vocab'), pairs)]]
    ppermute x16 -> x9, starting transfers between devices: 25.5 us -> 16.3 us  [swap(): return lax.ppermute(value, axis, [(i, i ^ k) for i in range(size)])]
    unnamed x16 -> x10, local copies, waits for them, and re-layouts: 7.38 us -> 0.03 us
    pallas_call x2 -> x12, Pallas kernels: 4.72 us -> 11.1 us  [the longest x3 5.02 us: fetched(): pl.pallas_call(functools.partial(fetch_kernel, start), in_specs=[pl.Block...]
    ppermute x0 -> x4, starting transfers between devices: none -> 6.26 us  [body(): pieces[n] = [total, lax.ppermute(total, ('dp', 'vocab'), pairs)]]
    concatenate x6 -> x0, other arithmetic: 2.21 us -> none  [doubled(): value = jnp.concatenate([value, swap(value, axis, size, k)], axis=0)]
    pallas_call x1, Pallas kernels: 5.53 us -> 4.33 us  [body(): pl.pallas_call(functools.partial(table_kernel, n_vocab, rows, bf16_terms(...]
  transfers between devices with their start and end apart: 16 -> 13, of which waited for: 10 -> 11; matrix products, arithmetic and copies ran while one was open for 0% -> 0% of each run, Pallas kernels for 12% -> 16%
where the time goes in v2:
time: 58.2 us; the launch traced here: 57.9 us
  starting transfers between devices  22.6 us (39%)
  waiting for transfers between devices  17.8 us (31%)
  Pallas kernels  16 us (27%)
  between operations  0.8 us (1%)
  other arithmetic  0.64 us (1%)
    ppermute x9, starting transfers between devices, swap(): return lax.ppermute(value, axis, [(i, i ^ k) for i in range(size)])  16.3 us
    ppermute x4, waiting for transfers between devices, body(): pieces[n] = [total, lax.ppermute(total, ('dp', 'vocab'), pairs)]  9.76 us
    ppermute x9, waiting for transfers between devices, swap(): return lax.ppermute(value, axis, [(i, i ^ k) for i in range(size)])  8.09 us
    ppermute x4, starting transfers between devices, body(): pieces[n] = [total, lax.ppermute(total, ('dp', 'vocab'), pairs)]  6.26 us
    pallas_call x3, Pallas kernels, fetched(): pl.pallas_call(functools.partial(fetch_kernel, start), in_specs=[pl.Block...  5.02 us
    pallas_call x1, Pallas kernels, body(): pl.pallas_call(functools.partial(table_kernel, n_vocab, rows, bf16_terms(...  4.33 us
    pallas_call x1, Pallas kernels, body(): pl.pallas_call(functools.partial(grad_kernel, n_vocab, rows, len(table)),...  2.17 us
    pallas_call x1, Pallas kernels, body(): pl.pallas_call(functools.partial(logits_fetch_kernel, tile, 2, 3 * quarte...  1.69 us
  transfers between devices with their start and end apart: 13, of which 11 were waited for; matrix products, arithmetic and copies ran while one was open for 0% of the time, Pallas kernels for 16%

profile of v2, /device:TPU:0, one launch (start us, length us, event | category | flops | bytes accessed | tf_op | source)
XLA Modules:
  0.0 57.9 jit_solution(469395106875609029)
XLA Ops:
  0.6 0.7 %paired.1.after_ref.refs_0_ = bf16[4,2304]{1,0:T(4,128)(2,1)S(1)} custom-call(bf16[4,1152]{1,0:T(4,128)(2,1)} %h_ref.1, bf16[4,1152]{1,0:T(4,128)(2,1)} %c_ref.1), custom_call_target="tpu_custom_call" | custom-call | tf_op jit(solution)/shard_map/paired/pallas_call | solution.py:72
  1.4 4.1 %collective-permute-start = (bf16[4,2304]{1,0:T(4,128)(2,1)S(1)}, bf16[4,2304]{1,0:T(4,128)(2,1)S(1)}, u32[]{:S(2)}, u32[]{:S(2)}) collective-permute-start(bf16[4,2304]{1,0:T(4,128)(2,1)S(1)} %paired.1.after_ref.refs_0_), channel_id=1, source_target_pairs={{0,4},{1,5},{2,6},{3,7},{4,0},{5,1},{6,2},{7,3},{8,12},{9,13},{10,... | collective-permute-start | bytes 55304 | tf_op jit(solution)/shard_map/ppermute | solution.py:21
  5.5 1.7 %fetched.3.refs_2_.refs_0_ = bf16[1024,1152]{1,0:T(8,128)(2,1)S(1)} custom-call(bf16[4096,1152]{1,0:T(8,128)(2,1)} %refs_2_.1, bf16[4,2304]{1,0:T(4,128)(2,1)S(1)} %paired.1.after_ref.refs_0_), custom_call_target="tpu_custom_call" | custom-call | bytes 4718592 | tf_op jit(solution)/shard_map/fetched/pallas_call | solution.py:115
  7.2 0.1 collective-permute-done.refs_1_
  7.3 2.0 %collective-permute-start.1 = (bf16[8,2304]{1,0:T(8,128)(2,1)S(1)}, bf16[8,2304]{1,0:T(8,128)(2,1)S(1)}, u32[]{:S(2)}, u32[]{:S(2)}) collective-permute-start(bf16[8,2304]{1,0:T(8,128)(2,1)S(1)} %joined.3.after_ref.refs_0_), channel_id=1, source_target_pairs={{0,2},{1,3},{2,0},{3,1},{4,6},{5,7},{6,4},{7,5},{8,10},{9,11},{10,... | collective-permute-start | bytes 110600 | tf_op jit(solution)/shard_map/ppermute | solution.py:21
  9.2 1.7 %fetched.4.refs_2_.refs_1_ = bf16[1024,1152]{1,0:T(8,128)(2,1)S(1)} custom-call(bf16[4096,1152]{1,0:T(8,128)(2,1)} %refs_2_.1, bf16[8,2304]{1,0:T(8,128)(2,1)S(1)} %joined.3.after_ref.refs_0_), custom_call_target="tpu_custom_call" | custom-call | bytes 4718592 | tf_op jit(solution)/shard_map/fetched/pallas_call | solution.py:115
  10.9 0.4 collective-permute-done.1.refs_1_
  11.3 0.0 collective-permute-start.2
  11.3 1.7 %fetched.5.refs_2_.refs_0_ = bf16[1024,1152]{1,0:T(8,128)(2,1)S(1)} custom-call(bf16[4096,1152]{1,0:T(8,128)(2,1)} %refs_2_.1, bf16[16,2304]{1,0:T(8,128)(2,1)S(1)} %joined.4.after_ref.refs_0_), custom_call_target="tpu_custom_call" | custom-call | bytes 4718592 | tf_op jit(solution)/shard_map/fetched/pallas_call | solution.py:115
  13.0 0.0 collective-permute-done.2.refs_1_
  13.0 1.7 %logits_a.1 = (f32[32,2048]{1,0:T(8,128)S(1)}, bf16[1024,1152]{1,0:T(8,128)(2,1)S(1)}) custom-call(bf16[32,2304]{1,0:T(8,128)(2,1)S(1)} %joined.5.h_ref.hc_ref, bf16[1024,1152]{1,0:T(8,128)(2,1)S(1)} %fetched.3.refs_2_.refs_0_, bf16[1024,1152]{1,0:T(8,128)(2,1)S(1)} %fetched.4.refs_2_.refs_1_, bf16[4096,1152]{1,0:T(8,128)(2,1)} %refs_2_.1), custom_call_target="tpu_custom_call" | custom-call | tf_op jit(solution)/shard_map/logits_a/pallas_call | solution.py:344
  14.7 0.0 copy-start
  14.7 1.4 %logits_b.1.a_ref = f32[32,2048]{1,0:T(8,128)S(1)} custom-call(bf16[32,2304]{1,0:T(8,128)(2,1)S(1)} %joined.5.h_ref.hc_ref, bf16[1024,1152]{1,0:T(8,128)(2,1)S(1)} %fetched.5.refs_2_.refs_0_, bf16[1024,1152]{1,0:T(8,128)(2,1)S(1)} %get-tuple-element.10.refs_1_.refs_3_), custom_call_target="tpu_custom_call" | custom-call | tf_op jit(solution)/shard_map/logits_b/pallas_call | solution.py:357
  16.1 0.0 copy-start.2
  16.1 0.0 copy-start.3
  16.2 2.0 %collective-permute-start.5 = (f32[32,2048]{1,0:T(8,128)S(1)}, f32[32,2048]{1,0:T(8,128)S(1)}, u32[]{:S(2)}, u32[]{:S(2)}) collective-permute-start(f32[32,2048]{1,0:T(8,128)S(1)} %logits_b.1.a_ref), channel_id=1, source_target_pairs={{0,8},{1,17},{2,10},{3,19},{4,12},{5,21},{6,14},{7,23},{8,0},{9,25... | collective-permute-start | bytes 786440 | tf_op jit(solution)/shard_map/ppermute | solution.py:377
  18.1 0.1 collective-permute-start.3
  18.2 4.3 %collective-permute-done.5.b_ref = f32[32,2048]{1,0:T(8,128)S(1)} collective-permute-done((f32[32,2048]{1,0:T(8,128)S(1)}, f32[32,2048]{1,0:T(8,128)S(1)}, u32[]{:S(2)}, u32[]{:S(2)}) %collective-permute-start.5) | collective-permute-done | bytes 262176 | tf_op jit(solution)/shard_map/ppermute | solution.py:377
  22.6 2.0 %collective-permute-start.6 = (f32[32,2048]{1,0:T(8,128)S(1)}, f32[32,2048]{1,0:T(8,128)S(1)}, u32[]{:S(2)}, u32[]{:S(2)}) collective-permute-start(f32[32,2048]{1,0:T(8,128)S(1)} %added.3.refs_2_), channel_id=1, source_target_pairs={{0,16},{1,9},{2,18},{3,11},{4,20},{5,13},{6,22},{7,15},{8,24},{9,1... | collective-permute-start | bytes 786440 | tf_op jit(solution)/shard_map/ppermute | solution.py:377
  24.6 1.1 %collective-permute-done.3.b_ref = f32[32,2048]{1,0:T(8,128)S(1)} collective-permute-done((f32[32,2048]{1,0:T(8,128)S(1)}, f32[32,2048]{1,0:T(8,128)S(1)}, u32[]{:S(2)}, u32[]{:S(2)}) %collective-permute-start.3) | collective-permute-done | bytes 262176 | tf_op jit(solution)/shard_map/ppermute | solution.py:377
  25.7 2.2 %collective-permute-start.4 = (f32[32,2048]{1,0:T(8,128)S(1)}, f32[32,2048]{1,0:T(8,128)S(1)}, u32[]{:S(2)}, u32[]{:S(2)}) collective-permute-start(f32[32,2048]{1,0:T(8,128)S(1)} %added.2.refs_0_), channel_id=1, source_target_pairs={{0,16},{1,9},{2,18},{3,11},{4,20},{5,13},{6,22},{7,15},{8,24},{9,1... | collective-permute-start | bytes 786440 | tf_op jit(solution)/shard_map/ppermute | solution.py:377
  27.9 1.2 %collective-permute-done.6.refs_3_ = f32[32,2048]{1,0:T(8,128)S(1)} collective-permute-done((f32[32,2048]{1,0:T(8,128)S(1)}, f32[32,2048]{1,0:T(8,128)S(1)}, u32[]{:S(2)}, u32[]{:S(2)}) %collective-permute-start.6) | collective-permute-done | bytes 262176 | tf_op jit(solution)/shard_map/ppermute | solution.py:377
  29.1 3.2 %collective-permute-done.4.refs_1_ = f32[32,2048]{1,0:T(8,128)S(1)} collective-permute-done((f32[32,2048]{1,0:T(8,128)S(1)}, f32[32,2048]{1,0:T(8,128)S(1)}, u32[]{:S(2)}, u32[]{:S(2)}) %collective-permute-start.4) | collective-permute-done | bytes 262176 | tf_op jit(solution)/shard_map/ppermute | solution.py:377
  32.2 0.0 copy-done
  32.2 0.3 stats.1
  32.6 3.1 %collective-permute-start.7 = (f32[8,128]{1,0:T(8,128)S(1)}, f32[8,128]{1,0:T(8,128)S(1)}, u32[]{:S(2)}, u32[]{:S(2)}) collective-permute-start(f32[8,128]{1,0:T(8,128)S(1)} %get-tuple-element.11.mine_ref), channel_id=1, source_target_pairs={{0,4},{1,5},{2,6},{3,7},{4,0},{5,1},{6,2},{7,3},{8,12},{9,13},{10,... | collective-permute-start | bytes 12296 | tf_op jit(solution)/shard_map/ppermute | solution.py:21
  35.7 1.6 %collective-permute-done.7.other_ref = f32[8,128]{1,0:T(8,128)S(1)} collective-permute-done((f32[8,128]{1,0:T(8,128)S(1)}, f32[8,128]{1,0:T(8,128)S(1)}, u32[]{:S(2)}, u32[]{:S(2)}) %collective-permute-start.7) | collective-permute-done | bytes 4128 | tf_op jit(solution)/shard_map/ppermute | solution.py:21
  37.3 0.1 join.3.mine_ref
  37.4 1.9 %collective-permute-start.8 = (f32[8,128]{1,0:T(8,128)S(1)}, f32[8,128]{1,0:T(8,128)S(1)}, u32[]{:S(2)}, u32[]{:S(2)}) collective-permute-start(f32[8,128]{1,0:T(8,128)S(1)} %join.3.mine_ref), channel_id=1, source_target_pairs={{0,2},{1,3},{2,0},{3,1},{4,6},{5,7},{6,4},{7,5},{8,10},{9,11},{10,... | collective-permute-start | bytes 12296 | tf_op jit(solution)/shard_map/ppermute | solution.py:21
  39.3 1.7 %collective-permute-done.8.other_ref = f32[8,128]{1,0:T(8,128)S(1)} collective-permute-done((f32[8,128]{1,0:T(8,128)S(1)}, f32[8,128]{1,0:T(8,128)S(1)}, u32[]{:S(2)}, u32[]{:S(2)}) %collective-permute-start.8) | collective-permute-done | bytes 4128 | tf_op jit(solution)/shard_map/ppermute | solution.py:21
  41.0 0.1 join.4.mine_ref
  41.1 0.0 collective-permute-start.9
  41.1 1.2 %collective-permute-done.9.other_ref = f32[8,128]{1,0:T(8,128)S(1)} collective-permute-done((f32[8,128]{1,0:T(8,128)S(1)}, f32[8,128]{1,0:T(8,128)S(1)}, u32[]{:S(2)}, u32[]{:S(2)}) %collective-permute-start.9) | collective-permute-done | bytes 4128 | tf_op jit(solution)/shard_map/ppermute | solution.py:21
  42.3 0.1 join.5.s_ref
  42.3 0.0 copy-done.1
  42.4 0.0 copy-done.2
  42.4 0.0 copy-done.3
  42.4 0.0 copy-start.4
  42.4 2.2 %grad.1 = (bf16[32,4096]{1,0:T(8,128)(2,1)S(1)}, f32[16,1152]{1,0:T(8,128)S(1)}, f32[16,1152]{1,0:T(8,128)S(1)}) custom-call(s32[1,32]{1,0:T(1,128)S(1)} %bitcast.6, s32[1,32]{1,0:T(1,128)S(1)} %bitcast.7, s32[1,8]{1,0:T(1,128)S(1)} %bitcast.8, s32[1,8]{1,0:T(1,128)S(1)} %bitcast.9, f32[8,128]{1,0:T(8,128)S(1)} %join.5.s_ref, ...), custom_call_target="tpu_custom_call" | custom-call | tf_op jit(solution)/shard_map/grad/pallas_call | solution.py:400
  44.6 0.2 collective-permute-start.10
  44.8 1.1 %collective-permute-done.10 = f32[16,1152]{1,0:T(8,128)S(1)} collective-permute-done((f32[16,1152]{1,0:T(8,128)S(1)}, f32[16,1152]{1,0:T(8,128)S(1)}, u32[]{:S(2)}, u32[]{:S(2)}) %collective-permute-start.10) | collective-permute-done | bytes 73760 | tf_op jit(solution)/shard_map/ppermute | solution.py:21
  45.9 1.9 %collective-permute-start.11 = (f32[8,1152]{1,0:T(8,128)S(1)}, f32[8,1152]{1,0:T(8,128)S(1)}, u32[]{:S(2)}, u32[]{:S(2)}) collective-permute-start(f32[8,1152]{1,0:T(8,128)S(1)} %get-tuple-element.17), channel_id=1, source_target_pairs={{0,2},{1,3},{2,0},{3,1},{4,6},{5,7},{6,4},{7,5},{8,10},{9,11},{10,... | collective-permute-start | bytes 110600 | tf_op jit(solution)/shard_map/ppermute | solution.py:21
  47.8 2.1 %collective-permute-done.11 = f32[8,1152]{1,0:T(8,128)S(1)} collective-permute-done((f32[8,1152]{1,0:T(8,128)S(1)}, f32[8,1152]{1,0:T(8,128)S(1)}, u32[]{:S(2)}, u32[]{:S(2)}) %collective-permute-start.11) | collective-permute-done | bytes 36896 | tf_op jit(solution)/shard_map/ppermute | solution.py:21
  49.9 3.0 %collective-permute-start.12 = (f32[4,1152]{1,0:T(4,128)S(1)}, f32[4,1152]{1,0:T(4,128)S(1)}, u32[]{:S(2)}, u32[]{:S(2)}) collective-permute-start(f32[4,1152]{1,0:T(4,128)S(1)} %slice_add_fusion.2), channel_id=1, source_target_pairs={{0,4},{1,5},{2,6},{3,7},{4,0},{5,1},{6,2},{7,3},{8,12},{9,13},{10,... | collective-permute-start | bytes 55304 | tf_op jit(solution)/shard_map/ppermute | solution.py:21
  52.9 0.0 copy-done.4
  52.9 4.3 %table.1 = bf16[4096,1152]{1,0:T(8,128)(2,1)} custom-call(s32[1,32]{1,0:T(1,128)S(1)} %bitcast.10, bf16[32,4096]{1,0:T(8,128)(2,1)S(1)} %get-tuple-element.13.g_ref, bf16[32,2304]{1,0:T(8,128)(2,1)S(1)} %joined.5.h_ref.hc_ref), custom_call_target="tpu_custom_call" | custom-call | flops 1207959552 | bytes 9437184 | tf_op jit(solution)/shard_map/table/pallas_call | solution.py:423
  57.3 0.0 collective-permute-done.12
  57.3 0.6 %fusion = f32[4,1152]{1,0:T(4,128)} fusion(f32[4,1152]{1,0:T(4,128)S(1)} %collective-permute-done.12, f32[8,1152]{1,0:T(8,128)S(1)} %collective-permute-done.11, f32[8,1152]{1,0:T(8,128)S(1)} %get-tuple-element.16), kind=kLoop, calls=%fused_computation.4 | loop fusion | flops 9216 | bytes 73728 | tf_op jit(solution)/shard_map/add | solution.py:421
  (8 shorter events, 0.1 us)
Async XLA Ops:
  1.4 5.9 %collective-permute-start = (bf16[4,2304]{1,0:T(4,128)(2,1)S(1)}, bf16[4,2304]{1,0:T(4,128)(2,1)S(1)}, u32[]{:S(2)}, u32[]{:S(2)}) collective-permute-start(bf16[4,2304]{1,0:T(4,128)(2,1)S(1)} %paired.1.after_ref.refs_0_), channel_id=1, source_target_pairs={{0,4},{1,5},{2,6},{3,7},{4,0},{5,1},{6,2},{7,3},{8,12},{9,13},{10,... | collective-permute-start | bytes 55304 | tf_op jit(solution)/shard_map/ppermute | solution.py:21
  7.3 4.0 %collective-permute-start.1 = (bf16[8,2304]{1,0:T(8,128)(2,1)S(1)}, bf16[8,2304]{1,0:T(8,128)(2,1)S(1)}, u32[]{:S(2)}, u32[]{:S(2)}) collective-permute-start(bf16[8,2304]{1,0:T(8,128)(2,1)S(1)} %joined.3.after_ref.refs_0_), channel_id=1, source_target_pairs={{0,2},{1,3},{2,0},{3,1},{4,6},{5,7},{6,4},{7,5},{8,10},{9,11},{10,... | collective-permute-start | bytes 110600 | tf_op jit(solution)/shard_map/ppermute | solution.py:21
  11.3 1.7 %collective-permute-start.2 = (bf16[16,2304]{1,0:T(8,128)(2,1)S(1)}, bf16[16,2304]{1,0:T(8,128)(2,1)S(1)}, u32[]{:S(2)}, u32[]{:S(2)}) collective-permute-start(bf16[16,2304]{1,0:T(8,128)(2,1)S(1)} %joined.4.after_ref.refs_0_), channel_id=1, source_target_pairs={{0,1},{1,0},{2,3},{3,2},{4,5},{5,4},{6,7},{7,6},{8,9},{9,8},{10,11... | collective-permute-start | bytes 221192 | tf_op jit(solution)/shard_map/ppermute | solution.py:21
  14.7 17.5 %copy-start = (s32[32]{0:T(128)S(1)}, s32[32]{0:T(128)}, u32[]{:S(2)}) copy-start(s32[32]{0:T(128)} %param.12) | copy-start | bytes 388
  16.1 26.2 %copy-start.1 = (s32[32]{0:T(128)S(1)}, s32[32]{0:T(128)}, u32[]{:S(2)}) copy-start(s32[32]{0:T(128)} %param.13) | copy-start | bytes 388
  16.1 26.2 %copy-start.2 = (s32[8]{0:T(128)S(1)}, s32[8]{0:T(128)}, u32[]{:S(2)}) copy-start(s32[8]{0:T(128)} %param.14) | copy-start | bytes 100
  16.1 26.2 %copy-start.3 = (s32[8]{0:T(128)S(1)}, s32[8]{0:T(128)}, u32[]{:S(2)}) copy-start(s32[8]{0:T(128)} %param.15) | copy-start | bytes 100
  16.2 6.4 %collective-permute-start.5 = (f32[32,2048]{1,0:T(8,128)S(1)}, f32[32,2048]{1,0:T(8,128)S(1)}, u32[]{:S(2)}, u32[]{:S(2)}) collective-permute-start(f32[32,2048]{1,0:T(8,128)S(1)} %logits_b.1.a_ref), channel_id=1, source_target_pairs={{0,8},{1,17},{2,10},{3,19},{4,12},{5,21},{6,14},{7,23},{8,0},{9,25... | collective-permute-start | bytes 786440 | tf_op jit(solution)/shard_map/ppermute | solution.py:377
  18.1 7.6 %collective-permute-start.3 = (f32[32,2048]{1,0:T(8,128)S(1)}, f32[32,2048]{1,0:T(8,128)S(1)}, u32[]{:S(2)}, u32[]{:S(2)}) collective-permute-start(f32[32,2048]{1,0:T(8,128)S(1)} %get-tuple-element.9.a_ref), channel_id=1, source_target_pairs={{0,8},{1,17},{2,10},{3,19},{4,12},{5,21},{6,14},{7,23},{8,0},{9,25... | collective-permute-start | bytes 786440 | tf_op jit(solution)/shard_map/ppermute | solution.py:377
  22.6 6.4 %collective-permute-start.6 = (f32[32,2048]{1,0:T(8,128)S(1)}, f32[32,2048]{1,0:T(8,128)S(1)}, u32[]{:S(2)}, u32[]{:S(2)}) collective-permute-start(f32[32,2048]{1,0:T(8,128)S(1)} %added.3.refs_2_), channel_id=1, source_target_pairs={{0,16},{1,9},{2,18},{3,11},{4,20},{5,13},{6,22},{7,15},{8,24},{9,1... | collective-permute-start | bytes 786440 | tf_op jit(solution)/shard_map/ppermute | solution.py:377
  25.7 6.5 %collective-permute-start.4 = (f32[32,2048]{1,0:T(8,128)S(1)}, f32[32,2048]{1,0:T(8,128)S(1)}, u32[]{:S(2)}, u32[]{:S(2)}) collective-permute-start(f32[32,2048]{1,0:T(8,128)S(1)} %added.2.refs_0_), channel_id=1, source_target_pairs={{0,16},{1,9},{2,18},{3,11},{4,20},{5,13},{6,22},{7,15},{8,24},{9,1... | collective-permute-start | bytes 786440 | tf_op jit(solution)/shard_map/ppermute | solution.py:377
  32.6 4.7 %collective-permute-start.7 = (f32[8,128]{1,0:T(8,128)S(1)}, f32[8,128]{1,0:T(8,128)S(1)}, u32[]{:S(2)}, u32[]{:S(2)}) collective-permute-start(f32[8,128]{1,0:T(8,128)S(1)} %get-tuple-element.11.mine_ref), channel_id=1, source_target_pairs={{0,4},{1,5},{2,6},{3,7},{4,0},{5,1},{6,2},{7,3},{8,12},{9,13},{10,... | collective-permute-start | bytes 12296 | tf_op jit(solution)/shard_map/ppermute | solution.py:21
  37.4 3.6 %collective-permute-start.8 = (f32[8,128]{1,0:T(8,128)S(1)}, f32[8,128]{1,0:T(8,128)S(1)}, u32[]{:S(2)}, u32[]{:S(2)}) collective-permute-start(f32[8,128]{1,0:T(8,128)S(1)} %join.3.mine_ref), channel_id=1, source_target_pairs={{0,2},{1,3},{2,0},{3,1},{4,6},{5,7},{6,4},{7,5},{8,10},{9,11},{10,... | collective-permute-start | bytes 12296 | tf_op jit(solution)/shard_map/ppermute | solution.py:21
  41.1 1.2 %collective-permute-start.9 = (f32[8,128]{1,0:T(8,128)S(1)}, f32[8,128]{1,0:T(8,128)S(1)}, u32[]{:S(2)}, u32[]{:S(2)}) collective-permute-start(f32[8,128]{1,0:T(8,128)S(1)} %join.4.mine_ref), channel_id=1, source_target_pairs={{0,1},{1,0},{2,3},{3,2},{4,5},{5,4},{6,7},{7,6},{8,9},{9,8},{10,11... | collective-permute-start | bytes 12296 | tf_op jit(solution)/shard_map/ppermute | solution.py:21
  42.4 10.6 %copy-start.4 = (s32[32]{0:T(128)S(1)}, s32[32]{0:T(128)}, u32[]{:S(2)}) copy-start(s32[32]{0:T(128)} %param.11) | copy-start | bytes 388
  44.6 1.3 %collective-permute-start.10 = (f32[16,1152]{1,0:T(8,128)S(1)}, f32[16,1152]{1,0:T(8,128)S(1)}, u32[]{:S(2)}, u32[]{:S(2)}) collective-permute-start(f32[16,1152]{1,0:T(8,128)S(1)} %get-tuple-element.15), channel_id=1, source_target_pairs={{0,1},{1,0},{2,3},{3,2},{4,5},{5,4},{6,7},{7,6},{8,9},{9,8},{10,11... | collective-permute-start | bytes 221192 | tf_op jit(solution)/shard_map/ppermute | solution.py:21
  45.9 4.0 %collective-permute-start.11 = (f32[8,1152]{1,0:T(8,128)S(1)}, f32[8,1152]{1,0:T(8,128)S(1)}, u32[]{:S(2)}, u32[]{:S(2)}) collective-permute-start(f32[8,1152]{1,0:T(8,128)S(1)} %get-tuple-element.17), channel_id=1, source_target_pairs={{0,2},{1,3},{2,0},{3,1},{4,6},{5,7},{6,4},{7,5},{8,10},{9,11},{10,... | collective-permute-start | bytes 110600 | tf_op jit(solution)/shard_map/ppermute | solution.py:21
  49.9 7.3 %collective-permute-start.12 = (f32[4,1152]{1,0:T(4,128)S(1)}, f32[4,1152]{1,0:T(4,128)S(1)}, u32[]{:S(2)}, u32[]{:S(2)}) collective-permute-start(f32[4,1152]{1,0:T(4,128)S(1)} %slice_add_fusion.2), channel_id=1, source_target_pairs={{0,4},{1,5},{2,6},{3,7},{4,0},{5,1},{6,2},{7,3},{8,12},{9,13},{10,... | collective-permute-start | bytes 55304 | tf_op jit(solution)/shard_map/ppermute | solution.py:21

commit v3 on v2

--- a/solution.py
+++ b/solution.py
@@ -173,46 +173,95 @@
     copy.wait()
 
 
-def stats_kernel(size, rows, parts, tgt_ref, *refs):
-    ins, (l_ref, s_ref) = refs[:-2], refs[-2:]
+def diagonal(rows, columns):
+    return lax.broadcasted_iota(jnp.int32, (rows, columns), 0) == lax.broadcasted_iota(
+        jnp.int32, (rows, columns), 1
+    )
+
+
+def soft_kernel(size, rows, parts, count, tgt_ref, *refs):
+    ins, e_refs = refs[: 2 * parts], refs[2 * parts : 2 * parts + count]
+    l_ref, keep_ref, send_ref, left_ref = refs[2 * parts + count :]
     tokens, width = l_ref.shape
+    depth = e_refs[0].shape[1]
     half = width // 2
     me = lax.axis_index("vocab")
-    picked = place_mask(me, tokens, rows, size)
-    target = ids_column(tgt_ref[...], picked)
+    target = ids_column(tgt_ref[...], place_mask(me, tokens, rows, size)) - me * width
     for n in range(2):
         total = ins[n * parts][...]
         for r in ins[n * parts + 1 : (n + 1) * parts]:
             total = total + r[...]
         l_ref[:, pl.ds(n * half, half)] = total
     logits = l_ref[...]
-    columns = lax.broadcasted_iota(jnp.int32, logits.shape, 1) + me * width
+    hit = lax.broadcasted_iota(jnp.int32, logits.shape, 1) == target
     top = jnp.max(logits, axis=1, keepdims=True)
-    total = jnp.sum(jnp.exp(logits - top), axis=1, keepdims=True)
-    pick = jnp.sum(jnp.where(columns == target, logits, 0.0), axis=1, keepdims=True)
-    same = lax.broadcasted_iota(jnp.int32, (tokens, s_ref.shape[1]), 0) == lax.broadcasted_iota(
-        jnp.int32, (tokens, s_ref.shape[1]), 1
-    )
-    s_ref[...] = jnp.zeros_like(s_ref)
-    for n, column in enumerate((top, total, pick)):
-        s_ref[n : n + 1, :] = jnp.sum(jnp.where(same, column, 0.0), axis=0, keepdims=True)
-
-
-def join_kernel(step, mine_ref, other_ref, out_ref):
-    width = mine_ref.shape[1]
-    other = other_ref[...]
-    lane = lax.broadcasted_iota(jnp.int32, other.shape, 1)
-    other = jnp.where(
-        (lane // step) % 2 == 1, pltpu.roll(other, step, 1), pltpu.roll(other, width - step, 1)
-    )
-    mine = mine_ref[...]
-    top = jnp.maximum(mine[0:1, :], other[0:1, :])
-    out_ref[...] = jnp.zeros_like(out_ref)
-    out_ref[0:1, :] = top
-    out_ref[1:2, :] = mine[1:2, :] * jnp.exp(mine[0:1, :] - top) + other[1:2, :] * jnp.exp(
-        other[0:1, :] - top
-    )
-    out_ref[2:3, :] = mine[2:3, :] + other[2:3, :]
+    share = jnp.exp(logits - top)
+    total = jnp.sum(share, axis=1, keepdims=True)
+    pick = jnp.sum(jnp.where(hit, logits, 0.0), axis=1, keepdims=True)
+    left_ref[:tokens, :] = jnp.where(hit, 0.0, share).astype(bf16)
+    left_ref[tokens:, :] = hit.astype(f32).astype(bf16)
+    part, at = None, 0
+    for e_ref in e_refs:
+        piece = jnp.dot(
+            left_ref[:, pl.ds(at, e_ref.shape[0])], e_ref[...], preferred_element_type=f32
+        )
+        part = piece if part is None else part + piece
+        at += e_ref.shape[0]
+    lanes = -(-tokens // LANES) * LANES
+    gap = (keep_ref.shape[1] - lanes) // 2
+    same = diagonal(tokens, lanes)
+    stats = [
+        jnp.sum(jnp.where(same, column, 0.0), axis=0, keepdims=True)
+        for column in (top, total, pick)
+    ]
+    n = tokens // 2
+    for at, ref in ((n, send_ref), (0, keep_ref)):
+        if gap != depth:
+            ref[...] = jnp.zeros_like(ref)
+        ref[:, :depth] = part[at : at + n]
+        ref[:, gap : gap + depth] = part[tokens + at : tokens + at + n]
+        ref[:, 2 * gap :] = jnp.zeros((n, lanes), f32)
+        for i, row in enumerate(stats):
+            ref[i : i + 1, 2 * gap :] = row
+
+
+def merged(step, lanes, mine_ref, other_ref):
+    count = mine_ref.shape[0]
+    gap = (mine_ref.shape[1] - lanes) // 2
+    lane = lax.broadcasted_iota(jnp.int32, (1, lanes), 1)
+
+    def aligned(row):
+        row = jnp.broadcast_to(row, (8, lanes))
+        turned = jnp.where(
+            (lax.broadcasted_iota(jnp.int32, row.shape, 1) // step) % 2 == 1,
+            pltpu.roll(row, step, 1),
+            pltpu.roll(row, lanes - step, 1),
+        )
+        return turned[0:1, :]
+
+    mine = [mine_ref[i : i + 1, 2 * gap :] for i in range(3)]
+    other = [aligned(other_ref[i : i + 1, 2 * gap :]) for i in range(3)]
+    top = jnp.maximum(mine[0], other[0])
+    scale_mine, scale_other = jnp.exp(mine[0] - top), jnp.exp(other[0] - top)
+    total = mine[1] * scale_mine + other[1] * scale_other
+    same = diagonal(count, lanes)
+    products = mine_ref[:, :gap] * as_column(scale_mine, same) + other_ref[
+        :, :gap
+    ] * as_column(scale_other, same)
+    rows = mine_ref[:, gap : 2 * gap] + other_ref[:, gap : 2 * gap]
+    return products, rows, (top, total, mine[2] + other[2])
+
+
+def join_kernel(step, lanes, mine_ref, other_ref, keep_ref, send_ref):
+    products, rows, stats = merged(step, lanes, mine_ref, other_ref)
+    n = keep_ref.shape[0]
+    gap = products.shape[1]
+    for at, ref in ((n, send_ref), (0, keep_ref)):
+        ref[:, :gap] = products[at : at + n]
+        ref[:, gap : 2 * gap] = rows[at : at + n]
+        ref[:, 2 * gap :] = jnp.zeros((n, lanes), f32)
+        for i, row in enumerate(stats):
+            ref[i : i + 1, 2 * gap :] = row
 
 
 def list_coef(scaled, lists, ranks):
@@ -233,42 +282,6 @@
     return preference_scale * (jnp.sum(portion, axis=0, keepdims=True) - 1.0)
 
 
-def grad_kernel(
-    size, rows, count, tgt_ref, seq_ref, list_ref, rank_ref, s_ref, l_ref, *refs
-):
-    e_refs, (g_ref, keep_ref, send_ref) = refs[:count], refs[count:]
-    tokens, width = l_ref.shape
-    seqs = list_ref.shape[1]
-    me = lax.axis_index("vocab")
-    picked = place_mask(me, tokens, rows, size)
-    target = ids_column(tgt_ref[...], picked)
-    seq = ids_column(seq_ref[...], picked)
-    same = lax.broadcasted_iota(jnp.int32, (tokens, s_ref.shape[1]), 0) == lax.broadcasted_iota(
-        jnp.int32, (tokens, s_ref.shape[1]), 1
-    )
-    top, total, pick = (as_column(s_ref[n : n + 1, :], same) for n in range(3))
-    log_norm = top + jnp.log(total)
-    seq_hot = seq == lax.broadcasted_iota(jnp.int32, (tokens, seqs), 1)
-    scores = jnp.sum(jnp.where(seq_hot, pick - log_norm, 0.0), axis=0, keepdims=True)
-    coef = list_coef(
-        preference_scale * scores, list_ref[...].astype(f32), rank_ref[...].astype(f32)
-    )
-    weight = as_column(coef, seq_hot)
-    logits = l_ref[...]
-    columns = lax.broadcasted_iota(jnp.int32, logits.shape, 1) + me * width
-    hit = (columns == target).astype(f32)
-    g_ref[...] = (weight * (hit - jnp.exp(logits - log_norm))).astype(bf16)
-    part, at = None, 0
-    for e_ref in e_refs:
-        piece = jnp.dot(
-            g_ref[:, pl.ds(at, e_ref.shape[0])], e_ref[...], preferred_element_type=f32
-        )
-        part = piece if part is None else part + piece
-        at += e_ref.shape[0]
-    keep_ref[...] = part[: tokens // 2]
-    send_ref[...] = part[tokens // 2 :]
-
-
 def bf16_terms(value, count=3):
     import numpy as np
 
@@ -280,29 +293,53 @@
     return terms
 
 
-def table_kernel(size, rows, terms, tile, ids_ref, g_ref, hc_ref, out_ref, buf, sems):
-    tokens, width = g_ref.shape
+def table_kernel(
+    size, rows, terms, tile, step,
+    tgt_ref, ids_ref, seq_ref, list_ref, rank_ref, mine_ref, other_ref, l_ref, hc_ref,
+    out_ref, hid_ref, buf, hid_buf, sems, hid_sem,
+):
+    tokens, width = l_ref.shape
     depth = out_ref.shape[1]
     gap = hc_ref.shape[1] // 2
+    lanes = mine_ref.shape[1] - 2 * gap
+    seqs = list_ref.shape[1]
     me = lax.axis_index("vocab")
-    ids = ids_column(ids_ref[...], place_mask(me, tokens, rows, size)) - me * width
+    picked = place_mask(me, tokens, rows, size)
+    target = ids_column(tgt_ref[...], picked) - me * width
+    ids = ids_column(ids_ref[...], picked) - me * width
+    seq = ids_column(seq_ref[...], picked)
+    products, hit_rows, stats = merged(step, lanes, mine_ref, other_ref)
+    same = diagonal(tokens, lanes)
+    top, total, pick = (as_column(row, same) for row in stats)
+    log_norm = top + jnp.log(total)
+    seq_hot = seq == lax.broadcasted_iota(jnp.int32, (tokens, seqs), 1)
+    scores = jnp.sum(jnp.where(seq_hot, pick - log_norm, 0.0), axis=0, keepdims=True)
+    coef = list_coef(
+        preference_scale * scores, list_ref[...].astype(f32), rank_ref[...].astype(f32)
+    )
+    weight = as_column(coef, seq_hot)
+    at_target = (weight * (1.0 - jnp.exp(pick - log_norm))).astype(bf16).astype(f32)
+    elsewhere = weight * jnp.exp(top - log_norm)
+    hid_buf[...] = (at_target[:rows] * hit_rows - elsewhere[:rows] * products)[:, :depth]
+    hid_copy = pltpu.make_async_copy(hid_buf, hid_ref, hid_sem)
+    hid_copy.start()
     right = jnp.concatenate(
         [hc_ref[:, :depth]] + [hc_ref[:, gap : gap + depth]] * len(terms), axis=0
     )
     copies = []
     for n in range(width // tile):
-        hit = lax.broadcasted_iota(jnp.int32, (tokens, tile), 1) + n * tile == ids
+        columns = lax.broadcasted_iota(jnp.int32, (tokens, tile), 1) + n * tile
+        share = jnp.exp(l_ref[:, pl.ds(n * tile, tile)] - log_norm)
+        grad = (weight * ((columns == target).astype(f32) - share)).astype(bf16)
+        hot = columns == ids
         left = jnp.concatenate(
-            [g_ref[:, pl.ds(n * tile, tile)]]
-            + [jnp.where(hit, t, 0.0).astype(bf16) for t in terms],
-            axis=0,
+            [grad] + [jnp.where(hot, t, 0.0).astype(bf16) for t in terms], axis=0
         )
-        buf[pl.ds(n * tile, tile), :] = lax.dot_general(
-            left, right, TN, preferred_element_type=f32
-        ).astype(bf16)
         at = pl.ds(n * tile, tile)
+        buf[at, :] = lax.dot_general(left, right, TN, preferred_element_type=f32).astype(bf16)
         copies.append(pltpu.make_async_copy(buf.at[at], out_ref.at[at], sems.at[n]))
         copies[-1].start()
+    hid_copy.wait()
     for copy in copies:
         copy.wait()
 
@@ -341,27 +378,29 @@
     both = after
     while len(fetches) < 3:
         fetches.append(fetched(embedding, len(fetches) * quarter, quarter, after))
-    part_a, last = pl.pallas_call(
-        functools.partial(logits_fetch_kernel, tile, 2, 3 * quarter),
-        in_specs=[VM] * 3 + [pl.BlockSpec(memory_space=pltpu.HBM)],
-        out_specs=(VM, VM),
-        out_shape=(
-            jax.ShapeDtypeStruct((tokens, half), f32),
-            jax.ShapeDtypeStruct((quarter, depth), bf16),
-        ),
-        scratch_shapes=[pltpu.SemaphoreType.DMA],
-        compiler_params=params(12),
-        name="logits_a",
-    )(both, *fetches[:2], embedding)
+    with jax.named_scope("logits_a"):
+        part_a, last = pl.pallas_call(
+            functools.partial(logits_fetch_kernel, tile, 2, 3 * quarter),
+            in_specs=[VM] * 3 + [pl.BlockSpec(memory_space=pltpu.HBM)],
+            out_specs=(VM, VM),
+            out_shape=(
+                jax.ShapeDtypeStruct((tokens, half), f32),
+                jax.ShapeDtypeStruct((quarter, depth), bf16),
+            ),
+            scratch_shapes=[pltpu.SemaphoreType.DMA],
+            compiler_params=params(12),
+            name="logits_a",
+        )(both, *fetches[:2], embedding)
     table = [*fetches, last]
-    part_b = pl.pallas_call(
-        functools.partial(logits_kernel, tile, 2),
-        in_specs=[VM] * 3,
-        out_specs=VM,
-        out_shape=jax.ShapeDtypeStruct((tokens, half), f32),
-        compiler_params=params(12),
-        name="logits_b",
-    )(both, *table[2:])
+    with jax.named_scope("logits_b"):
+        part_b = pl.pallas_call(
+            functools.partial(logits_kernel, tile, 2),
+            in_specs=[VM] * 3,
+            out_specs=VM,
+            out_shape=jax.ShapeDtypeStruct((tokens, half), f32),
+            compiler_params=params(12),
+            name="logits_b",
+        )(both, *table[2:])
 
     order = halvings(n_dp)[::-1]
     pieces = [[part_a], [part_b]]
@@ -374,68 +413,59 @@
         ]
         for n in range(2):
             total = added(pieces[n])
-            pieces[n] = [total, lax.ppermute(total, ("dp", "vocab"), pairs)]
+            with jax.named_scope(f"dp_{n}_{r}"):
+                pieces[n] = [total, lax.ppermute(total, ("dp", "vocab"), pairs)]
     parts = len(pieces[0])
-    logits, stats = pl.pallas_call(
-        functools.partial(stats_kernel, n_vocab, rows, parts),
-        in_specs=[VM] * (1 + 2 * parts),
-        out_specs=(VM, VM),
+    packed = 2 * gap + lanes
+    logits, keep, send = pl.pallas_call(
+        functools.partial(soft_kernel, n_vocab, rows, parts, len(table)),
+        in_specs=[VM] * (1 + 2 * parts + len(table)),
+        out_specs=(VM, VM, VM),
         out_shape=(
             jax.ShapeDtypeStruct((tokens, width), f32),
-            jax.ShapeDtypeStruct((8, lanes), f32),
+            jax.ShapeDtypeStruct((tokens // 2, packed), f32),
+            jax.ShapeDtypeStruct((tokens // 2, packed), f32),
         ),
-        compiler_params=params(12),
-        name="stats",
-    )(tgt, *pieces[0], *pieces[1])
-    for r, k in enumerate(halvings(n_vocab)):
-        stats = pl.pallas_call(
-            functools.partial(join_kernel, rows << r),
-            in_specs=[VM, VM],
-            out_specs=VM,
-            out_shape=jax.ShapeDtypeStruct(stats.shape, f32),
-            compiler_params=params(2),
-            name="join",
-        )(stats, swap(stats, "vocab", n_vocab, k))
-
-    grad, keep, send = pl.pallas_call(
-        functools.partial(grad_kernel, n_vocab, rows, len(table)),
-        in_specs=[VM] * (6 + len(table)),
-        out_specs=(VM, VM, VM),
-        out_shape=(
-            jax.ShapeDtypeStruct((tokens, width), bf16),
-            jax.ShapeDtypeStruct((tokens // 2, depth), f32),
-            jax.ShapeDtypeStruct((tokens // 2, depth), f32),
-        ),
-        compiler_params=params(12),
-        name="grad",
-    )(tgt, seq, lists, ranks, stats, logits, *table)
+        scratch_shapes=[pltpu.VMEM((2 * tokens, width), bf16)],
+        compiler_params=params(14),
+        name="soft",
+    )(tgt, *pieces[0], *pieces[1], *table)
 
     back = halvings(n_vocab)[::-1]
     for n, k in enumerate(back):
         other = swap(send, "vocab", n_vocab, k)
+        step = rows * (n_vocab >> (n + 1))
         if n + 1 < len(back):
-            cut = keep.shape[0] // 2
-            send = keep[cut:] + other[cut:]
-            keep = keep[:cut] + other[:cut]
-        else:
-            keep = keep + other
+            shape = jax.ShapeDtypeStruct((keep.shape[0] // 2, packed), f32)
+            keep, send = pl.pallas_call(
+                functools.partial(join_kernel, step, lanes),
+                in_specs=[VM, VM],
+                out_specs=(VM, VM),
+                out_shape=(shape, shape),
+                compiler_params=params(4),
+                name="join",
+            )(keep, other)
     block = math.gcd(512, width)
-    table_grad = pl.pallas_call(
-        functools.partial(table_kernel, n_vocab, rows, bf16_terms(math.sqrt(width_all)), block),
-        in_specs=[VM, VM, VM],
-        out_specs=pl.BlockSpec(memory_space=pltpu.HBM),
-        out_shape=jax.ShapeDtypeStruct((width, depth), bf16),
+    hbm = pl.BlockSpec(memory_space=pltpu.HBM)
+    return pl.pallas_call(
+        functools.partial(
+            table_kernel, n_vocab, rows, bf16_terms(math.sqrt(width_all)), block, step
+        ),
+        in_specs=[VM] * 9,
+        out_specs=(hbm, hbm),
+        out_shape=(
+            jax.ShapeDtypeStruct((width, depth), bf16),
+            jax.ShapeDtypeStruct((rows, depth), f32),
+        ),
         scratch_shapes=[
             pltpu.VMEM((width, depth), bf16),
+            pltpu.VMEM((rows, depth), f32),
             pltpu.SemaphoreType.DMA((width // block,)),
+            pltpu.SemaphoreType.DMA,
         ],
         compiler_params=params(24),
-        cost_estimate=pl.CostEstimate(
-            flops=2 * 128 * width * depth, bytes_accessed=2 * width * depth, transcendentals=0
-        ),
         name="table",
-    )(ids, grad, both)
-    return (table_grad, keep)
+    )(tgt, ids, seq, lists, ranks, keep, other, logits, both)
 
 
 def solution(mesh):

time: 58.2 us -> 50.7 us (0.87)
  starting transfers between devices: 22.6 us -> 17.3 us
  waiting for transfers between devices: 17.8 us -> 16.3 us
  other arithmetic: 0.64 us -> 0 us
    ppermute x9 -> x6, starting transfers between devices: 16.3 us -> 11.1 us  [swap(): return lax.ppermute(value, axis, [(i, i ^ k) for i in range(size)])]
    ppermute x9 -> x6, waiting for transfers between devices: 8.09 us -> 6.56 us  [swap(): return lax.ppermute(value, axis, [(i, i ^ k) for i in range(size)])]
    add x3 -> x0, other arithmetic: 0.64 us -> none  [the longest x1 0.62 us: body(): keep = keep + other]
    pallas_call x5 -> x3, Pallas kernels: 2.75 us -> 2.28 us  [the longest x1 1.96 us: body(): pl.pallas_call(functools.partial(soft_kernel, n_vocab, rows, parts, len(t...]
  transfers between devices with their start and end apart: 13 -> 10, of which waited for: 11 -> 9; matrix products, arithmetic and copies ran while one was open for 0% -> 0% of each run, Pallas kernels for 16% -> 10%
where the time goes in v3:
time: 50.7 us; the launch traced here: 50.5 us
  starting transfers between devices  17.3 us (34%)
  waiting for transfers between devices  16.3 us (32%)
  Pallas kernels  16 us (32%)
  between operations  0.77 us (2%)
    ppermute x6, starting transfers between devices, swap(): return lax.ppermute(value, axis, [(i, i ^ k) for i in range(size)])  11.1 us
    ppermute x4, waiting for transfers between devices, body(): pieces[n] = [total, lax.ppermute(total, ('dp', 'vocab'), pairs)]  9.76 us
    ppermute x6, waiting for transfers between devices, swap(): return lax.ppermute(value, axis, [(i, i ^ k) for i in range(size)])  6.56 us
    ppermute x4, starting transfers between devices, body(): pieces[n] = [total, lax.ppermute(total, ('dp', 'vocab'), pairs)]  6.25 us
    pallas_call x3, Pallas kernels, fetched(): pl.pallas_call(functools.partial(fetch_kernel, start), in_specs=[pl.Block...  5.02 us
    pallas_call x1, Pallas kernels, body(): pl.pallas_call(functools.partial(table_kernel, n_vocab, rows, bf16_terms(...  4.79 us
    pallas_call x1, Pallas kernels, body(): pl.pallas_call(functools.partial(soft_kernel, n_vocab, rows, parts, len(t...  1.96 us
    pallas_call x1, Pallas kernels, body(): pl.pallas_call(functools.partial(logits_fetch_kernel, tile, 2, 3 * quarte...  1.69 us
  transfers between devices with their start and end apart: 10, of which 9 were waited for; matrix products, arithmetic and copies ran while one was open for 0% of the time, Pallas kernels for 10%

profile of v3, /device:TPU:0, one launch (start us, length us, event | category | flops | bytes accessed | tf_op | source)
XLA Modules:
  0.0 50.5 jit_solution(12094665485337229066)
XLA Ops:
  0.6 0.7 %paired.1.after_ref.refs_0_ = bf16[4,2304]{1,0:T(4,128)(2,1)S(1)} custom-call(bf16[4,1152]{1,0:T(4,128)(2,1)} %h_ref.1, bf16[4,1152]{1,0:T(4,128)(2,1)} %c_ref.1), custom_call_target="tpu_custom_call" | custom-call | tf_op jit(solution)/shard_map/paired/pallas_call | solution.py:72
  1.4 4.1 %collective-permute-start = (bf16[4,2304]{1,0:T(4,128)(2,1)S(1)}, bf16[4,2304]{1,0:T(4,128)(2,1)S(1)}, u32[]{:S(2)}, u32[]{:S(2)}) collective-permute-start(bf16[4,2304]{1,0:T(4,128)(2,1)S(1)} %paired.1.after_ref.refs_0_), channel_id=1, source_target_pairs={{0,4},{1,5},{2,6},{3,7},{4,0},{5,1},{6,2},{7,3},{8,12},{9,13},{10,... | collective-permute-start | bytes 55304 | tf_op jit(solution)/shard_map/ppermute | solution.py:21
  5.5 1.7 %fetched.3.refs_2_.refs_0_.refs_4_ = bf16[1024,1152]{1,0:T(8,128)(2,1)S(1)} custom-call(bf16[4096,1152]{1,0:T(8,128)(2,1)} %refs_2_.1, bf16[4,2304]{1,0:T(4,128)(2,1)S(1)} %paired.1.after_ref.refs_0_), custom_call_target="tpu_custom_call" | custom-call | bytes 4718592 | tf_op jit(solution)/shard_map/fetched/pallas_call | solution.py:115
  7.2 0.1 collective-permute-done.refs_1_
  7.3 2.0 %collective-permute-start.1 = (bf16[8,2304]{1,0:T(8,128)(2,1)S(1)}, bf16[8,2304]{1,0:T(8,128)(2,1)S(1)}, u32[]{:S(2)}, u32[]{:S(2)}) collective-permute-start(bf16[8,2304]{1,0:T(8,128)(2,1)S(1)} %joined.3.after_ref.refs_0_), channel_id=1, source_target_pairs={{0,2},{1,3},{2,0},{3,1},{4,6},{5,7},{6,4},{7,5},{8,10},{9,11},{10,... | collective-permute-start | bytes 110600 | tf_op jit(solution)/shard_map/ppermute | solution.py:21
  9.2 1.7 %fetched.4.refs_2_.refs_1_.refs_5_ = bf16[1024,1152]{1,0:T(8,128)(2,1)S(1)} custom-call(bf16[4096,1152]{1,0:T(8,128)(2,1)} %refs_2_.1, bf16[8,2304]{1,0:T(8,128)(2,1)S(1)} %joined.3.after_ref.refs_0_), custom_call_target="tpu_custom_call" | custom-call | bytes 4718592 | tf_op jit(solution)/shard_map/fetched/pallas_call | solution.py:115
  10.9 0.4 collective-permute-done.1.refs_1_
  11.3 0.0 collective-permute-start.2
  11.3 1.7 %fetched.5.refs_2_.refs_0_.refs_6_ = bf16[1024,1152]{1,0:T(8,128)(2,1)S(1)} custom-call(bf16[4096,1152]{1,0:T(8,128)(2,1)} %refs_2_.1, bf16[16,2304]{1,0:T(8,128)(2,1)S(1)} %joined.4.after_ref.refs_0_), custom_call_target="tpu_custom_call" | custom-call | bytes 4718592 | tf_op jit(solution)/shard_map/fetched/pallas_call | solution.py:115
  13.0 0.0 collective-permute-done.2.refs_1_
  13.0 1.7 %logits_a.1 = (f32[32,2048]{1,0:T(8,128)S(1)}, bf16[1024,1152]{1,0:T(8,128)(2,1)S(1)}) custom-call(bf16[32,2304]{1,0:T(8,128)(2,1)S(1)} %joined.5.h_ref.hc_ref, bf16[1024,1152]{1,0:T(8,128)(2,1)S(1)} %fetched.3.refs_2_.refs_0_.refs_4_, bf16[1024,1152]{1,0:T(8,128)(2,1)S(1)} %fetched.4.refs_2_.refs_1_.refs_5_, bf16[4096,1152]{1,0:T(8,128)(2,1)} %refs_2_.1), custom_call_target="tpu_custom_call" | custom-call | tf_op jit(solution)/shard_map/logits_a/logits_a/pallas_call | solution.py:382
  14.7 0.0 copy-start
  14.7 1.4 %logits_b.1.a_ref = f32[32,2048]{1,0:T(8,128)S(1)} custom-call(bf16[32,2304]{1,0:T(8,128)(2,1)S(1)} %joined.5.h_ref.hc_ref, bf16[1024,1152]{1,0:T(8,128)(2,1)S(1)} %fetched.5.refs_2_.refs_0_.refs_6_, bf16[1024,1152]{1,0:T(8,128)(2,1)S(1)} %get-tuple-element.12.refs_1_.refs_7_), custom_call_target="tpu_custom_call" | custom-call | tf_op jit(solution)/shard_map/logits_b/logits_b/pallas_call | solution.py:396
  16.1 2.0 %collective-permute-start.5 = (f32[32,2048]{1,0:T(8,128)S(1)}, f32[32,2048]{1,0:T(8,128)S(1)}, u32[]{:S(2)}, u32[]{:S(2)}) collective-permute-start(f32[32,2048]{1,0:T(8,128)S(1)} %logits_b.1.a_ref), channel_id=1, source_target_pairs={{0,8},{1,17},{2,10},{3,19},{4,12},{5,21},{6,14},{7,23},{8,0},{9,25... | collective-permute-start | bytes 786440 | tf_op jit(solution)/shard_map/dp_1_0/ppermute | solution.py:417
  18.1 0.1 collective-permute-start.3
  18.2 4.3 %collective-permute-done.5.b_ref = f32[32,2048]{1,0:T(8,128)S(1)} collective-permute-done((f32[32,2048]{1,0:T(8,128)S(1)}, f32[32,2048]{1,0:T(8,128)S(1)}, u32[]{:S(2)}, u32[]{:S(2)}) %collective-permute-start.5) | collective-permute-done | bytes 262176 | tf_op jit(solution)/shard_map/dp_1_0/ppermute | solution.py:417
  22.6 2.0 %collective-permute-start.6 = (f32[32,2048]{1,0:T(8,128)S(1)}, f32[32,2048]{1,0:T(8,128)S(1)}, u32[]{:S(2)}, u32[]{:S(2)}) collective-permute-start(f32[32,2048]{1,0:T(8,128)S(1)} %added.3.refs_2_), channel_id=1, source_target_pairs={{0,16},{1,9},{2,18},{3,11},{4,20},{5,13},{6,22},{7,15},{8,24},{9,1... | collective-permute-start | bytes 786440 | tf_op jit(solution)/shard_map/dp_1_1/ppermute | solution.py:417
  24.6 1.1 %collective-permute-done.3.b_ref = f32[32,2048]{1,0:T(8,128)S(1)} collective-permute-done((f32[32,2048]{1,0:T(8,128)S(1)}, f32[32,2048]{1,0:T(8,128)S(1)}, u32[]{:S(2)}, u32[]{:S(2)}) %collective-permute-start.3) | collective-permute-done | bytes 262176 | tf_op jit(solution)/shard_map/dp_0_0/ppermute | solution.py:417
  25.7 2.2 %collective-permute-start.4 = (f32[32,2048]{1,0:T(8,128)S(1)}, f32[32,2048]{1,0:T(8,128)S(1)}, u32[]{:S(2)}, u32[]{:S(2)}) collective-permute-start(f32[32,2048]{1,0:T(8,128)S(1)} %added.2.refs_0_), channel_id=1, source_target_pairs={{0,16},{1,9},{2,18},{3,11},{4,20},{5,13},{6,22},{7,15},{8,24},{9,1... | collective-permute-start | bytes 786440 | tf_op jit(solution)/shard_map/dp_0_1/ppermute | solution.py:417
  27.9 1.2 %collective-permute-done.6.refs_3_ = f32[32,2048]{1,0:T(8,128)S(1)} collective-permute-done((f32[32,2048]{1,0:T(8,128)S(1)}, f32[32,2048]{1,0:T(8,128)S(1)}, u32[]{:S(2)}, u32[]{:S(2)}) %collective-permute-start.6) | collective-permute-done | bytes 262176 | tf_op jit(solution)/shard_map/dp_1_1/ppermute | solution.py:417
  29.0 3.2 %collective-permute-done.4.refs_1_ = f32[32,2048]{1,0:T(8,128)S(1)} collective-permute-done((f32[32,2048]{1,0:T(8,128)S(1)}, f32[32,2048]{1,0:T(8,128)S(1)}, u32[]{:S(2)}, u32[]{:S(2)}) %collective-permute-start.4) | collective-permute-done | bytes 262176 | tf_op jit(solution)/shard_map/dp_0_1/ppermute | solution.py:417
  32.2 0.0 copy-done
  32.2 0.0 copy-start.1
  32.2 0.0 copy-start.2
  32.2 0.0 copy-start.3
  32.2 0.0 copy-start.4
  32.2 2.0 %soft.1 = (f32[32,4096]{1,0:T(8,128)S(1)}, f32[16,2432]{1,0:T(8,128)S(1)}, f32[16,2432]{1,0:T(8,128)S(1)}) custom-call(s32[1,32]{1,0:T(1,128)S(1)} %bitcast.5, f32[32,2048]{1,0:T(8,128)S(1)} %added.2.refs_0_, f32[32,2048]{1,0:T(8,128)S(1)} %collective-permute-done.4.refs_1_, f32[32,2048]{1,0:T(8,128)S(1)} %added.3.refs_2_, ...), custom_call_target="tpu_custom_call" | custom-call | tf_op jit(solution)/shard_map/soft/pallas_call | solution.py:420
  34.2 0.1 collective-permute-start.7
  34.3 1.4 %collective-permute-done.7.other_ref = f32[16,2432]{1,0:T(8,128)S(1)} collective-permute-done((f32[16,2432]{1,0:T(8,128)S(1)}, f32[16,2432]{1,0:T(8,128)S(1)}, u32[]{:S(2)}, u32[]{:S(2)}) %collective-permute-start.7) | collective-permute-done | bytes 155680 | tf_op jit(solution)/shard_map/ppermute | solution.py:21
  35.6 0.2 join.2
  35.8 2.1 %collective-permute-start.8 = (f32[8,2432]{1,0:T(8,128)S(1)}, f32[8,2432]{1,0:T(8,128)S(1)}, u32[]{:S(2)}, u32[]{:S(2)}) collective-permute-start(f32[8,2432]{1,0:T(8,128)S(1)} %get-tuple-element.16), channel_id=1, source_target_pairs={{0,2},{1,3},{2,0},{3,1},{4,6},{5,7},{6,4},{7,5},{8,10},{9,11},{10,... | collective-permute-start | bytes 233480 | tf_op jit(solution)/shard_map/ppermute | solution.py:21
  37.9 2.7 %collective-permute-done.8.other_ref = f32[8,2432]{1,0:T(8,128)S(1)} collective-permute-done((f32[8,2432]{1,0:T(8,128)S(1)}, f32[8,2432]{1,0:T(8,128)S(1)}, u32[]{:S(2)}, u32[]{:S(2)}) %collective-permute-start.8) | collective-permute-done | bytes 77856 | tf_op jit(solution)/shard_map/ppermute | solution.py:21
  40.6 0.2 join.3
  40.7 2.8 %collective-permute-start.9 = (f32[4,2432]{1,0:T(4,128)S(1)}, f32[4,2432]{1,0:T(4,128)S(1)}, u32[]{:S(2)}, u32[]{:S(2)}) collective-permute-start(f32[4,2432]{1,0:T(4,128)S(1)} %get-tuple-element.18), channel_id=1, source_target_pairs={{0,4},{1,5},{2,6},{3,7},{4,0},{5,1},{6,2},{7,3},{8,12},{9,13},{10,... | collective-permute-start | bytes 116744 | tf_op jit(solution)/shard_map/ppermute | solution.py:21
  43.6 2.1 %collective-permute-done.9.other_ref = f32[4,2432]{1,0:T(4,128)S(1)} collective-permute-done((f32[4,2432]{1,0:T(4,128)S(1)}, f32[4,2432]{1,0:T(4,128)S(1)}, u32[]{:S(2)}, u32[]{:S(2)}) %collective-permute-start.9) | collective-permute-done | bytes 38944 | tf_op jit(solution)/shard_map/ppermute | solution.py:21
  45.6 0.0 copy-done.1
  45.6 0.0 copy-done.2
  45.7 0.0 copy-done.3
  45.7 0.0 copy-done.4
  45.7 4.8 %table.1 = (bf16[4096,1152]{1,0:T(8,128)(2,1)}, f32[4,1152]{1,0:T(4,128)}) custom-call(s32[1,32]{1,0:T(1,128)S(1)} %bitcast.6, s32[1,32]{1,0:T(1,128)S(1)} %bitcast.7, s32[1,32]{1,0:T(1,128)S(1)} %bitcast.8, s32[1,8]{1,0:T(1,128)S(1)} %bitcast.9, s32[1,8]{1,0:T(1,128)S(1)} %bitcast.10, f32[4,2432]{1,0:T(4,128)S(1)} %get-tuple-element.17.mine_ref, ...), custom_call_target="tpu_custom_call" | custom-call | tf_op jit(solution)/shard_map/table/pallas_call | solution.py:450
  (5 shorter events, 0.1 us)
Async XLA Ops:
  1.4 5.9 %collective-permute-start = (bf16[4,2304]{1,0:T(4,128)(2,1)S(1)}, bf16[4,2304]{1,0:T(4,128)(2,1)S(1)}, u32[]{:S(2)}, u32[]{:S(2)}) collective-permute-start(bf16[4,2304]{1,0:T(4,128)(2,1)S(1)} %paired.1.after_ref.refs_0_), channel_id=1, source_target_pairs={{0,4},{1,5},{2,6},{3,7},{4,0},{5,1},{6,2},{7,3},{8,12},{9,13},{10,... | collective-permute-start | bytes 55304 | tf_op jit(solution)/shard_map/ppermute | solution.py:21
  7.3 4.0 %collective-permute-start.1 = (bf16[8,2304]{1,0:T(8,128)(2,1)S(1)}, bf16[8,2304]{1,0:T(8,128)(2,1)S(1)}, u32[]{:S(2)}, u32[]{:S(2)}) collective-permute-start(bf16[8,2304]{1,0:T(8,128)(2,1)S(1)} %joined.3.after_ref.refs_0_), channel_id=1, source_target_pairs={{0,2},{1,3},{2,0},{3,1},{4,6},{5,7},{6,4},{7,5},{8,10},{9,11},{10,... | collective-permute-start | bytes 110600 | tf_op jit(solution)/shard_map/ppermute | solution.py:21
  11.3 1.7 %collective-permute-start.2 = (bf16[16,2304]{1,0:T(8,128)(2,1)S(1)}, bf16[16,2304]{1,0:T(8,128)(2,1)S(1)}, u32[]{:S(2)}, u32[]{:S(2)}) collective-permute-start(bf16[16,2304]{1,0:T(8,128)(2,1)S(1)} %joined.4.after_ref.refs_0_), channel_id=1, source_target_pairs={{0,1},{1,0},{2,3},{3,2},{4,5},{5,4},{6,7},{7,6},{8,9},{9,8},{10,11... | collective-permute-start | bytes 221192 | tf_op jit(solution)/shard_map/ppermute | solution.py:21
  14.7 17.5 %copy-start = (s32[32]{0:T(128)S(1)}, s32[32]{0:T(128)}, u32[]{:S(2)}) copy-start(s32[32]{0:T(128)} %param.12) | copy-start | bytes 388
  16.1 6.4 %collective-permute-start.5 = (f32[32,2048]{1,0:T(8,128)S(1)}, f32[32,2048]{1,0:T(8,128)S(1)}, u32[]{:S(2)}, u32[]{:S(2)}) collective-permute-start(f32[32,2048]{1,0:T(8,128)S(1)} %logits_b.1.a_ref), channel_id=1, source_target_pairs={{0,8},{1,17},{2,10},{3,19},{4,12},{5,21},{6,14},{7,23},{8,0},{9,25... | collective-permute-start | bytes 786440 | tf_op jit(solution)/shard_map/dp_1_0/ppermute | solution.py:417
  18.1 7.6 %collective-permute-start.3 = (f32[32,2048]{1,0:T(8,128)S(1)}, f32[32,2048]{1,0:T(8,128)S(1)}, u32[]{:S(2)}, u32[]{:S(2)}) collective-permute-start(f32[32,2048]{1,0:T(8,128)S(1)} %get-tuple-element.11.a_ref), channel_id=1, source_target_pairs={{0,8},{1,17},{2,10},{3,19},{4,12},{5,21},{6,14},{7,23},{8,0},{9,25... | collective-permute-start | bytes 786440 | tf_op jit(solution)/shard_map/dp_0_0/ppermute | solution.py:417
  22.6 6.4 %collective-permute-start.6 = (f32[32,2048]{1,0:T(8,128)S(1)}, f32[32,2048]{1,0:T(8,128)S(1)}, u32[]{:S(2)}, u32[]{:S(2)}) collective-permute-start(f32[32,2048]{1,0:T(8,128)S(1)} %added.3.refs_2_), channel_id=1, source_target_pairs={{0,16},{1,9},{2,18},{3,11},{4,20},{5,13},{6,22},{7,15},{8,24},{9,1... | collective-permute-start | bytes 786440 | tf_op jit(solution)/shard_map/dp_1_1/ppermute | solution.py:417
  25.7 6.5 %collective-permute-start.4 = (f32[32,2048]{1,0:T(8,128)S(1)}, f32[32,2048]{1,0:T(8,128)S(1)}, u32[]{:S(2)}, u32[]{:S(2)}) collective-permute-start(f32[32,2048]{1,0:T(8,128)S(1)} %added.2.refs_0_), channel_id=1, source_target_pairs={{0,16},{1,9},{2,18},{3,11},{4,20},{5,13},{6,22},{7,15},{8,24},{9,1... | collective-permute-start | bytes 786440 | tf_op jit(solution)/shard_map/dp_0_1/ppermute | solution.py:417
  32.2 13.4 %copy-start.1 = (s32[32]{0:T(128)S(1)}, s32[32]{0:T(128)}, u32[]{:S(2)}) copy-start(s32[32]{0:T(128)} %param.11) | copy-start | bytes 388
  32.2 13.4 %copy-start.2 = (s32[32]{0:T(128)S(1)}, s32[32]{0:T(128)}, u32[]{:S(2)}) copy-start(s32[32]{0:T(128)} %param.13) | copy-start | bytes 388
  32.2 13.4 %copy-start.3 = (s32[8]{0:T(128)S(1)}, s32[8]{0:T(128)}, u32[]{:S(2)}) copy-start(s32[8]{0:T(128)} %param.14) | copy-start | bytes 100
  32.2 13.4 %copy-start.4 = (s32[8]{0:T(128)S(1)}, s32[8]{0:T(128)}, u32[]{:S(2)}) copy-start(s32[8]{0:T(128)} %param.15) | copy-start | bytes 100
  34.2 1.4 %collective-permute-start.7 = (f32[16,2432]{1,0:T(8,128)S(1)}, f32[16,2432]{1,0:T(8,128)S(1)}, u32[]{:S(2)}, u32[]{:S(2)}) collective-permute-start(f32[16,2432]{1,0:T(8,128)S(1)} %get-tuple-element.14), channel_id=1, source_target_pairs={{0,1},{1,0},{2,3},{3,2},{4,5},{5,4},{6,7},{7,6},{8,9},{9,8},{10,11... | collective-permute-start | bytes 466952 | tf_op jit(solution)/shard_map/ppermute | solution.py:21
  35.8 4.7 %collective-permute-start.8 = (f32[8,2432]{1,0:T(8,128)S(1)}, f32[8,2432]{1,0:T(8,128)S(1)}, u32[]{:S(2)}, u32[]{:S(2)}) collective-permute-start(f32[8,2432]{1,0:T(8,128)S(1)} %get-tuple-element.16), channel_id=1, source_target_pairs={{0,2},{1,3},{2,0},{3,1},{4,6},{5,7},{6,4},{7,5},{8,10},{9,11},{10,... | collective-permute-start | bytes 233480 | tf_op jit(solution)/shard_map/ppermute | solution.py:21
  40.7 4.9 %collective-permute-start.9 = (f32[4,2432]{1,0:T(4,128)S(1)}, f32[4,2432]{1,0:T(4,128)S(1)}, u32[]{:S(2)}, u32[]{:S(2)}) collective-permute-start(f32[4,2432]{1,0:T(4,128)S(1)} %get-tuple-element.18), channel_id=1, source_target_pairs={{0,4},{1,5},{2,6},{3,7},{4,0},{5,1},{6,2},{7,3},{8,12},{9,13},{10,... | collective-permute-start | bytes 116744 | tf_op jit(solution)/shard_map/ppermute | solution.py:21
